TPU v7x, 256 devices: a whole 4x4x8 slice. The times are simulated.
256 devices in a mesh: blk: 8 (over x_hi, y), rep: 32 (over z, x_lo, core).
Axes of the slice: x: 4 (x_hi: 2, x_lo: 2; x = x_hi * 2 + x_lo), y: 4, z: 8, core: 2. Of those that a mesh axis runs over, the one named last changes fastest.
Arguments:
- query_hidden: bfloat16 [32, 32, 32, 768], P('rep', 'blk'), may hold values from -18 to 18
- passage_hidden: bfloat16 [32, 32, 512, 768], P('rep', 'blk'), may hold values from -6 to 6
- lengths: int32 [32, 32], P('rep', 'blk'), may hold values from 64 to 512
- projection: bfloat16 [768, 128], replicated, may hold values from -0.21875 to 0.21875
Outputs:
- query_grad: float32 [32, 32, 32, 128], P('rep', 'blk')
- passage_grad: float32 [32, 32, 512, 128], P('rep', 'blk')
- grad_weight: float32 [768, 128], replicated
- loss: float32 [], replicated
All inputs are finite; a program needn't handle non-finite values.
Results may differ from a plain program's by a relative error of at most 0.0097.
Values may be sent and summed in bfloat16 or wider, within the bound.
No kernel may reach another device: no remote copies, remote signals or barrier semaphores. Data moves between devices by JAX's collectives and lax.ppermute only.
A program may use at most 128 MiB of HBM per device.

v0:
```python
import jax
import jax.numpy as jnp
from jax import lax
from jax.sharding import PartitionSpec as P

temper = 0.5


def soft_scores(scores, lens):
    slots = scores.shape[-1]
    valid = lax.broadcasted_iota(jnp.int32, (lens.shape[0], slots), 1) < lens[:, None]
    scaled = jnp.where(valid[None], scores / temper, -jnp.inf)
    top = jnp.max(scaled, -1, keepdims=True)
    logz = top + jnp.log(jnp.sum(jnp.exp(scaled - top), -1, keepdims=True))
    pooled = temper * (logz[..., 0] - jnp.log(lens.astype(jnp.float32))[None])
    return (pooled, scaled, logz)


def cross_entropy(score, first, total):
    top = jnp.max(score, 1, keepdims=True)
    lse = top + jnp.log(jnp.sum(jnp.exp(score - top), 1, keepdims=True))
    target = lax.broadcasted_iota(jnp.int32, score.shape, 1) == first + lax.broadcasted_iota(
        jnp.int32, score.shape, 0
    )
    loss_part = jnp.sum(lse[:, 0] - jnp.sum(jnp.where(target, score, 0.0), 1))
    dscore = (jnp.exp(score - lse) - target.astype(jnp.float32)) / total
    return (loss_part, dscore)


def weighted(dscore, scaled, logz, qlen):
    spread = jnp.repeat(dscore, qlen, axis=0)
    grad_a = (spread[:, :, None] * jnp.exp(scaled - logz)).astype(jnp.bfloat16)
    return grad_a.reshape(grad_a.shape[0], -1)


def shards(query_hidden, passage_hidden, lengths, projection):
    hidden = projection.shape[0]
    nquery = query_hidden.shape[1]
    qlen = query_hidden.shape[2]
    npass = passage_hidden.shape[1]
    plen = passage_hidden.shape[2]
    groups = lax.axis_size("blk")
    total = groups * lax.axis_size("rep") * nquery
    first = lax.axis_index("blk") * nquery
    qflat = query_hidden[0].reshape(-1, hidden)
    pflat = passage_hidden[0].reshape(-1, hidden)
    qtok = jnp.dot(qflat, projection, preferred_element_type=jnp.float32).astype(jnp.bfloat16)
    ptok = jnp.dot(pflat, projection, preferred_element_type=jnp.float32).astype(jnp.bfloat16)
    every_tok = lax.all_gather(ptok, "blk", axis=0, tiled=True)
    every_len = lax.all_gather(lengths[0], "blk", axis=0, tiled=True)
    scores = jnp.dot(qtok, every_tok.T, preferred_element_type=jnp.float32).reshape(
        nquery * qlen, groups * npass, plen
    )
    pooled, scaled, logz = soft_scores(scores, every_len)
    score = jnp.sum(pooled.reshape(nquery, qlen, groups * npass), 1)
    loss_part, dscore = cross_entropy(score, first, total)
    grad_a = weighted(dscore, scaled, logz, qlen)
    qgrad = jnp.dot(grad_a, every_tok, preferred_element_type=jnp.float32)
    pgrad = lax.psum_scatter(
        jnp.dot(grad_a.T, qtok, preferred_element_type=jnp.float32),
        "blk",
        scatter_dimension=0,
        tiled=True,
    )
    wgrad = jnp.dot(qflat.T, qgrad.astype(jnp.bfloat16), preferred_element_type=jnp.float32)
    wgrad = wgrad + jnp.dot(pflat.T, pgrad.astype(jnp.bfloat16), preferred_element_type=jnp.float32)
    wgrad, loss_sum = lax.psum((wgrad, loss_part), ("blk", "rep"))
    query_grad = qgrad.reshape(1, nquery, qlen, -1)
    passage_grad = pgrad.reshape(1, npass, plen, -1)
    return (query_grad, passage_grad, wgrad, loss_sum / total)


def solution(mesh):
    return jax.shard_map(
        shards,
        mesh=mesh,
        in_specs=(P("rep", "blk", None, None), P("rep", "blk", None, None), P("rep", "blk"), P()),
        out_specs=(P("rep", "blk", None, None), P("rep", "blk", None, None), P(), P()),
        check_vma=False,
    )
```

profile of v0, /device:TPU:1, one launch (start us, length us, event | category | flops | bytes accessed | tf_op | source)
XLA Modules:
  0.0 521.1 jit_solution(17235841440828739490)
XLA Ops:
  7.2 0.0 copy-start
  7.2 0.0 all-gather.3.cloned.1.call-start
  7.2 1.8 copy-done
  9.1 2.7 convolution_convert_fusion
  11.8 0.0 all-gather.3.cloned.1.call-update
  11.8 0.0 reduce-scatter.2.cloned.1.call-start
  11.9 1.3 dynamic-slice
  13.8 0.8 bitcast_dynamic-update-slice_fusion
  14.6 11.6 %all-reduce = s32[32]{0:T(128)S(1)} all-reduce(s32[32]{0:T(128)S(1)} %bitcast_dynamic-update-slice_fusion), channel_id=2, replica_groups=mesh['blk'=8,'rep'=32] {'blk'}, use_global_device_ids=true, to_apply=%add | all-reduce | flops 32 | bytes 256 | tf_op jit(solution)/shard_map/all_gather | solution.py:50
  26.2 0.1 lt.21
  26.3 0.1 iota_compare_fusion
  26.4 1.2 convolution_convert_fusion.1
  27.6 64.1 %all-gather.3.cloned.1.call-done = bf16[16384,128]{1,0:T(8,128)(2,1)} async-done(((bf16[2048,128]{1,0:T(8,128)(2,1)}), bf16[16384,128]{1,0:T(8,128)(2,1)}) %all-gather.3.cloned.1.call-update) | async-done | bytes 4194320 | tf_op jit(solution)/shard_map/all_gather | solution.py:49
  91.8 3.4 convolution_multiply_fusion
  95.2 0.0 copy-start.1
  95.2 6.5 %copy.9 = f32[16,8,32,512]{3,2,1,0:T(8,128)S(1)} copy(f32[16,8,32,512]{3,1,2,0:T(8,128)S(1)} %bitcast.36) | data formatting | bytes 16777216
  101.8 0.0 copy-done.1
  101.8 0.7 select_reduce_fusion
  102.5 2.3 exponential_reduce_fusion
  104.8 0.1 reduce_max.19
  104.9 0.2 select_reduce_fusion.1
  105.1 0.6 subtract_reduce_fusion
  105.7 0.1 subtract_multiply_fusion
  105.8 0.7 mul.27
  106.5 9.7 %copy.10 = f32[16,8,32,512]{3,1,2,0:T(8,128)} copy(f32[16,8,32,512]{3,2,1,0:T(8,128)S(1)} %bitcast.43) | data formatting | bytes 16777216
  116.2 0.0 slice-start
  116.2 0.9 sub.59
  117.2 0.0 slice-start.1
  117.2 9.8 %copy.12 = f32[16,8,32,512]{3,1,2,0:T(8,128)} copy(f32[16,8,32,512]{3,2,1,0:T(8,128)S(1)} %bitcast.44) | data formatting | bytes 16777216
  126.9 0.0 slice-done
  126.9 0.0 slice-done.1
  126.9 7.0 %multiply_convert_fusion = bf16[128,16384]{1,0:T(8,128)(2,1)S(1)} fusion(f32[128,16384]{1,0:T(8,128)} %bitcast.41, f32[128,16384]{1,0:T(8,128)} %bitcast.42, f32[128,16384]{1,0:T(8,128)S(1)} %bitcast.38, pred[16384]{0:T(1024)(128)(4,1)S(1)} %lt.23), kind=kLoop, calls=%fused_computation.1 | loop fusion | flops 8388608 | bytes 29376512 | tf_op jit(solution)/shard_map/convert_element_type | solution.py:32
  134.0 0.0 copy-start.2
  134.0 2.0 copy-done.2
  136.0 4.5 fusion.5
  140.5 0.0 reduce-scatter.2.cloned.1.call-update
  140.5 0.0 copy-start.3
  140.5 0.0 all-reduce.3.cloned.1.call-start
  140.6 4.7 fusion.4
  145.3 0.0 copy-start.4
  145.3 112.7 %reduce-scatter.2.cloned.1.call-done = f32[2048,128]{1,0:T(8,128)} async-done(((f32[16384,128]{1,0:T(8,128)}), f32[2048,128]{1,0:T(8,128)}) %reduce-scatter.2.cloned.1.call-update) | async-done | bytes 1048592 | tf_op jit(solution)/shard_map/reduce_scatter | solution.py:59
  258.1 1.8 fusion.1
  259.9 0.0 copy-done.3
  259.9 1.0 fusion
  260.9 0.0 all-reduce.3.cloned.1.call-update
  260.9 74.6 %psum.15 = f32[]{:T(128)} all-reduce(f32[]{:T(128)} %get-tuple-element.10), channel_id=1, replica_groups=mesh['blk'=8,'rep'=32] {'blk','rep'}, use_global_device_ids=true, to_apply=%region_9.10 | all-reduce | flops 1 | bytes 8 | tf_op jit(solution)/shard_map/psum | solution.py:67
  336.2 175.4 %all-reduce.3.cloned.1.call-done = f32[768,128]{0,1:T(8,128)} async-done(((f32[768,128]{0,1:T(8,128)}), f32[768,128]{0,1:T(8,128)}) %all-reduce.3.cloned.1.call-update) | async-done | bytes 393232 | tf_op jit(solution)/shard_map/psum | solution.py:67
  511.5 1.9 copy.8
  513.4 0.0 copy-done.4
  (9 shorter events, 0.1 us)
Async XLA Ops:
  7.2 1.9 copy-start
  7.2 84.6 %all-gather.3.cloned.1.call-start = ((), (), s32[]{:S(2)}) async-start(), calls=%async_computation.1 | async-start | bytes 4718592 | tf_op jit(solution)/shard_map/all_gather | solution.py:49
  11.8 246.3 %reduce-scatter.2.cloned.1.call-start = ((), (), s32[]{:S(2)}) async-start(), calls=%async_computation.2 | async-start | bytes 9437184 | tf_op jit(solution)/shard_map/reduce_scatter | solution.py:59
  95.2 6.5 %copy-start.1 = (f32[128,16384]{1,0:T(8,128)}, f32[128,16384]{1,0:T(8,128)S(1)}, u32[]{:S(2)}) copy-start(f32[128,16384]{1,0:T(8,128)S(1)} %convolution_multiply_fusion) | copy-start | bytes 25165828
  116.2 10.7 %slice-start = ((s8[8388608]{0:T(1024)(128)(4,1)}), s8[4194304]{0:T(1024)(128)(4,1)S(1)}, s32[]{:S(2)}) async-start(s8[8388608]{0:T(1024)(128)(4,1)} %bitcast.37), calls=%async_computation.4 | async-start | bytes 8388608
  117.2 9.8 %slice-start.1 = ((s8[8388608]{0:T(1024)(128)(4,1)}), s8[4194304]{0:T(1024)(128)(4,1)S(1)}, s32[]{:S(2)}) async-start(s8[8388608]{0:T(1024)(128)(4,1)} %bitcast.37), calls=%async_computation.5 | async-start | bytes 8388608
  134.0 2.0 copy-start.2
  140.5 119.4 %copy-start.3 = (bf16[1,4,32,768]{3,2,1,0:T(8,128)(2,1)S(1)}, bf16[1,4,32,768]{3,2,1,0:T(8,128)(2,1)}, u32[]{:S(2)}) copy-start(bf16[1,4,32,768]{3,2,1,0:T(8,128)(2,1)} %param.4) | copy-start | bytes 589828
  140.5 371.0 %all-reduce.3.cloned.1.call-start = ((), (), s32[]{:S(2)}) async-start(), calls=%async_computation.3 | async-start | bytes 786432 | tf_op jit(solution)/shard_map/psum | solution.py:67
  145.3 368.1 %copy-start.4 = (f32[128,128]{1,0:T(8,128)}, f32[128,128]{1,0:T(8,128)S(1)}, u32[]{:S(2)}) copy-start(f32[128,128]{1,0:T(8,128)S(1)} %fusion.4) | copy-start | bytes 196612
Sparse Core Ops, SparseCore 0:
  11.9 79.8 all-gather.2
  140.6 117.3 reduce-scatter.1
  265.1 246.4 all-reduce.2
where the time goes:
time: 522 us; the launch traced here: 521 us
  waiting for transfers between devices  352 us (67%)
  blocking collectives  86.2 us (17%)
  local copies, waits for them, and re-layouts  35.5 us (7%)
  matrix products  19.4 us (4%)
  between operations  16.4 us (3%)
  other arithmetic  11.2 us (2%)
    psum x1, waiting for transfers between devices, shards(): wgrad, loss_sum = lax.psum((wgrad, loss_part), ('blk', 'rep'))  175 us
    reduce_scatter x1, waiting for transfers between devices, shards(): lax.psum_scatter(jnp.dot(grad_a.T, qtok, preferred_element_type=jnp.float...  113 us
    psum x1, blocking collectives, shards(): wgrad, loss_sum = lax.psum((wgrad, loss_part), ('blk', 'rep'))  74.6 us
    all_gather x1, waiting for transfers between devices, shards(): every_tok = lax.all_gather(ptok, 'blk', axis=0, tiled=True)  64.1 us
    unnamed x23, local copies, waits for them, and re-layouts  33.8 us
    all_gather x1, blocking collectives, shards(): every_len = lax.all_gather(lengths[0], 'blk', axis=0, tiled=True)  11.6 us
  transfers between devices with their start and end apart: 3, of which 3 were waited for; matrix products, arithmetic and copies ran while one was open for 2% of the time, Pallas kernels for 0%

commit v1 on v0

v1 whole, which is shorter than its diff:
```python
import functools
import math

import jax
import jax.numpy as jnp
from jax import lax
from jax.experimental import pallas as pl
from jax.experimental.pallas import tpu as pltpu
from jax.sharding import PartitionSpec as P

F32 = jnp.float32
BF16 = jnp.bfloat16
INV_TEMPER = 2.0
TEMPER = 0.5
LANES = 128
EXTRA = 32
NN = (((1,), (0,)), ((), ()))
NT = (((1,), (1,)), ((), ()))
TN = (((0,), (0,)), ((), ()))


def mm(a, b, dims):
    return lax.dot_general(a, b, dims, preferred_element_type=F32)


def to_row(x):
    return jnp.concatenate([x[c : c + 1, :] for c in range(x.shape[0])], axis=1)


def to_chunks(x):
    n = x.shape[1] // LANES
    return jnp.concatenate([x[:, c * LANES : (c + 1) * LANES] for c in range(n)], axis=0)


def split3(x):
    hi = x.astype(BF16).astype(F32)
    rest = x - hi
    mid = rest.astype(BF16).astype(F32)
    return hi, mid, (rest - mid)


def segment_sum(x, width):
    lane = lax.broadcasted_iota(jnp.int32, x.shape, 1)
    step = 1
    while step < width:
        up = pltpu.roll(x, x.shape[1] - step, 1)
        down = pltpu.roll(x, step, 1)
        x = x + jnp.where((lane & step) == 0, up, down)
        step *= 2
    return x


def query_kernel(q_ref, w_ref, out_ref):
    tok = mm(q_ref[...], w_ref[...], NN)
    flipped = tok.T.astype(BF16)
    for c in range(out_ref.shape[0]):
        out_ref[c] = flipped


def score_kernel(qlen, len_ref, me_ref, qt_ref, phid_ref, w_ref, e_ref, stat_ref, send_ref, own_ref, qs_ref, g_ref):
    p = pl.program_id(0)
    nblk = qt_ref.shape[0]
    slots = phid_ref.shape[1]
    npass = stat_ref.shape[1]

    @pl.when(p == 0)
    def _():
        for c in range(nblk):
            qs_ref[:, c * LANES : (c + 1) * LANES] = qt_ref[c]

    ptok = mm(phid_ref[0], w_ref[...], NN)
    pvec = ptok.astype(BF16)
    pvec_t = ptok.T.astype(BF16)
    count = len_ref[p]
    scores = mm(pvec, qs_ref[...], NN)
    row = lax.broadcasted_iota(jnp.int32, scores.shape, 0)
    scores = jnp.where(row < count, scores, -jnp.inf)
    top = jnp.max(scores, axis=0, keepdims=True)
    e = jnp.exp2((scores - top) * (INV_TEMPER * math.log2(math.e)))
    total = jnp.sum(e, axis=0, keepdims=True)
    eb = e.astype(BF16)
    e_ref[0] = eb
    inv = 1.0 / total
    g = mm(pvec_t, eb, NN) * inv
    for c in range(nblk):
        g_ref[p, c] = g[:, c * LANES : (c + 1) * LANES]
    logz = to_chunks(top * INV_TEMPER + jnp.log(total))
    log_count = jnp.log(jnp.full(logz.shape, count, jnp.int32).astype(F32))
    stat_ref[0, p] = segment_sum(TEMPER * (logz - log_count), qlen)
    stat_ref[1, p] = to_chunks(inv)

    @pl.when(p == npass - 1)
    def _():
        score = [stat_ref[0, k] for k in range(npass)]
        high = functools.reduce(jnp.maximum, score)
        lse = high + jnp.log(sum(jnp.exp(s - high) for s in score))
        share = [jnp.exp(s - lse) for s in score]
        hi, mid, lo = split3(lse)
        extra = jnp.concatenate([hi, mid, lo, jnp.zeros_like(lo)], axis=0).astype(BF16)
        for c in range(nblk):
            part = sum(g_ref[k, c] * share[k][c : c + 1, :] for k in range(npass))
            send_ref[c, :LANES, :] = part.astype(BF16)
            send_ref[c, LANES:, :] = extra
        me = me_ref[0]
        for k in range(npass):
            own_ref[k] = g_ref[k, me]


def grad_kernel(
    qlen, total, len_ref, me_ref, recv_ref, e_ref, stat_ref, own_ref, qt_ref, phid_ref, qhid_ref,
    qgrad_ref, pgrad_ref, send_ref, lse_ref, acc_ref, qs_ref,
):
    p = pl.program_id(0)
    nblk = qt_ref.shape[0]
    npass = stat_ref.shape[1]
    me = me_ref[0]
    lane = lax.broadcasted_iota(jnp.int32, (nblk, LANES), 1)
    chunk = lax.broadcasted_iota(jnp.int32, (nblk, LANES), 0)
    mine = chunk == me

    def pick(x):
        return jnp.sum(jnp.where(mine, x, 0.0), axis=0, keepdims=True)

    def dscore_of(k, lse):
        hit = mine & (lane // qlen == k)
        return (jnp.exp(stat_ref[0, k] - lse) - hit.astype(F32)) / total

    @pl.when(p == 0)
    def _():
        parts = []
        for d in range(nblk):
            x = recv_ref[d, LANES:, :].astype(F32)
            parts.append(x[:nblk] + x[nblk : 2 * nblk] + x[2 * nblk : 3 * nblk])
        high = functools.reduce(jnp.maximum, parts)
        lse = high + jnp.log(sum(jnp.exp(x - high) for x in parts))
        lse_ref[...] = lse
        grad = jnp.zeros((LANES, LANES), F32)
        for k in range(npass):
            grad = grad + own_ref[k] * pick(dscore_of(k, lse))
        for d in range(nblk):
            share = jnp.where(me == d, 0.0, pick(jnp.exp(parts[d] - lse)) / total)
            grad = grad + recv_ref[d, :LANES, :].astype(F32) * share
        grad = grad.T
        qgrad_ref[...] = grad
        acc_ref[...] = mm(qhid_ref[...], grad.astype(BF16), TN)

    lse = lse_ref[...]
    weight = dscore_of(p, lse) * stat_ref[1, p]
    for c in range(nblk):
        qs_ref[:, c * LANES : (c + 1) * LANES] = (qt_ref[c].astype(F32) * weight[c : c + 1, :]).astype(BF16)
    pgrad = mm(e_ref[0], qs_ref[...], NT)
    pgrad_ref[0] = pgrad
    acc_ref[...] += mm(phid_ref[0], pgrad.astype(BF16), TN)

    @pl.when(p == npass - 1)
    def _():
        loss = jnp.zeros((nblk, LANES), F32)
        for k in range(npass):
            first = mine & (lane == k * qlen)
            loss = loss + jnp.where(first, lse - stat_ref[0, k], 0.0)
        hi, mid, lo = split3(jnp.full((1, LANES), jnp.sum(loss)))
        extra = jnp.concatenate([hi, mid, lo, jnp.zeros((5, LANES), F32)], axis=0)
        nrep, rows = send_ref.shape[0], send_ref.shape[1] - 8
        for r in range(nrep):
            send_ref[r] = jnp.concatenate([acc_ref[r * rows : (r + 1) * rows, :], extra], axis=0).astype(BF16)


def sum_spread_kernel(x_ref, out_ref):
    y = jnp.sum(x_ref[...].astype(F32), axis=0)
    for c in range(out_ref.shape[0]):
        out_ref[c] = y


def sum_final_kernel(total, x_ref, out_ref, loss_ref):
    y = jnp.sum(x_ref[...], axis=0)
    rows = out_ref.shape[1]
    z = y[:rows].astype(BF16)
    for c in range(out_ref.shape[0]):
        out_ref[c] = z
    loss_ref[...] = jnp.sum(y[rows:], axis=0, keepdims=True) / total


def params(mib=48):
    return pltpu.CompilerParams(vmem_limit_bytes=mib << 20)


VM = pl.BlockSpec(memory_space=pltpu.VMEM)
SM = pl.BlockSpec(memory_space=pltpu.SMEM)


def whole(shape):
    return pl.BlockSpec(shape, lambda p: (0,) * len(shape))


def shards(query_hidden, passage_hidden, lengths, projection):
    hidden, dim = projection.shape
    nquery, qlen = query_hidden.shape[1:3]
    npass, plen = passage_hidden.shape[1:3]
    nblk, nrep = lax.axis_size("blk"), lax.axis_size("rep")
    total = nblk * nrep * nquery
    ntok = nblk * nquery * qlen
    qflat = query_hidden[0].reshape(-1, hidden)
    phid = passage_hidden[0]
    lens = lengths[0]
    me = lax.axis_index("blk").astype(jnp.int32)[None]

    copies = pl.pallas_call(
        query_kernel,
        name="query_tokens",
        out_shape=jax.ShapeDtypeStruct((nblk, dim, nquery * qlen), BF16),
        in_specs=[VM, VM],
        out_specs=VM,
        compiler_params=params(),
    )(qflat, projection)
    qt = lax.all_to_all(copies, "blk", 0, 0)

    e, stat, send, own = pl.pallas_call(
        functools.partial(score_kernel, qlen),
        name="scores",
        grid=(npass,),
        out_shape=(
            jax.ShapeDtypeStruct((npass, plen, ntok), BF16),
            jax.ShapeDtypeStruct((2, npass, nblk, LANES), F32),
            jax.ShapeDtypeStruct((nblk, dim + EXTRA, LANES), BF16),
            jax.ShapeDtypeStruct((npass, dim, LANES), F32),
        ),
        in_specs=[
            SM,
            SM,
            whole((nblk, dim, LANES)),
            pl.BlockSpec((1, plen, hidden), lambda p: (p, 0, 0)),
            whole((hidden, dim)),
        ],
        out_specs=(
            pl.BlockSpec((1, plen, ntok), lambda p: (p, 0, 0)),
            whole((2, npass, nblk, LANES)),
            whole((nblk, dim + EXTRA, LANES)),
            whole((npass, dim, LANES)),
        ),
        scratch_shapes=[pltpu.VMEM((dim, ntok), BF16), pltpu.VMEM((npass, nblk, dim, LANES), F32)],
        compiler_params=params(),
    )(lens, me, qt, phid, projection)
    recv = lax.all_to_all(send, "blk", 0, 0)

    rows = hidden // nrep
    qgrad, pgrad, send = pl.pallas_call(
        functools.partial(grad_kernel, qlen, float(total)),
        name="grads",
        grid=(npass,),
        out_shape=(
            jax.ShapeDtypeStruct((nquery * qlen, dim), F32),
            jax.ShapeDtypeStruct((npass, plen, dim), F32),
            jax.ShapeDtypeStruct((nrep, rows + 8, dim), BF16),
        ),
        in_specs=[
            SM,
            SM,
            whole((nblk, dim + EXTRA, LANES)),
            pl.BlockSpec((1, plen, ntok), lambda p: (p, 0, 0)),
            whole((2, npass, nblk, LANES)),
            whole((npass, dim, LANES)),
            whole((nblk, dim, LANES)),
            pl.BlockSpec((1, plen, hidden), lambda p: (p, 0, 0)),
            whole((nquery * qlen, hidden)),
        ],
        out_specs=(
            whole((nquery * qlen, dim)),
            pl.BlockSpec((1, plen, dim), lambda p: (p, 0, 0)),
            whole((nrep, rows + 8, dim)),
        ),
        scratch_shapes=[
            pltpu.VMEM((nblk, LANES), F32),
            pltpu.VMEM((hidden, dim), F32),
            pltpu.VMEM((dim, ntok), BF16),
        ],
        compiler_params=params(),
    )(lens, me, recv, e, stat, own, qt, phid, qflat)

    part = lax.all_to_all(send, "rep", 0, 0)
    part = pl.pallas_call(
        sum_spread_kernel,
        name="sum_rep",
        out_shape=jax.ShapeDtypeStruct((nblk, rows + 8, dim), F32),
        in_specs=[VM],
        out_specs=VM,
        compiler_params=params(),
    )(part)
    part = lax.all_to_all(part, "blk", 0, 0)
    part, loss = pl.pallas_call(
        functools.partial(sum_final_kernel, float(total)),
        name="sum_blk",
        out_shape=(jax.ShapeDtypeStruct((nrep, rows, dim), BF16), jax.ShapeDtypeStruct((1, dim), F32)),
        in_specs=[VM],
        out_specs=(VM, VM),
        compiler_params=params(),
    )(part)
    wgrad = lax.all_to_all(part, "rep", 0, 0).astype(F32).reshape(hidden, dim)
    return (
        qgrad.reshape(1, nquery, qlen, dim),
        pgrad.reshape(1, npass, plen, dim),
        wgrad,
        loss[0, 0],
    )


def solution(mesh):
    return jax.shard_map(
        shards,
        mesh=mesh,
        in_specs=(P("rep", "blk", None, None), P("rep", "blk", None, None), P("rep", "blk"), P()),
        out_specs=(P("rep", "blk", None, None), P("rep", "blk", None, None), P(), P()),
        check_vma=False,
    )
```

time: 522 us -> 99.1 us (0.19)
  waiting for transfers between devices: 352 us -> 7.58 us
  local copies, waits for them, and re-layouts: 35.5 us -> 5.32 us
  blocking collectives: 86.2 us -> 58.9 us
  matrix products: 19.4 us -> 0 us
  Pallas kernels: 0 us -> 17.8 us
  between operations: 16.4 us -> 0.65 us
  other arithmetic: 11.2 us -> 0.79 us
  starting transfers between devices: 0.12 us -> 7.48 us
    psum x1 -> x0, waiting for transfers between devices: 175 us -> none  [shards(): wgrad, loss_sum = lax.psum((wgrad, loss_part), ('blk', 'rep'))]
    reduce_scatter x1 -> x0, waiting for transfers between devices: 113 us -> none  [shards(): lax.psum_scatter(jnp.dot(grad_a.T, qtok, preferred_element_type=jnp.float...]
    psum x1 -> x0, blocking collectives: 74.6 us -> none  [shards(): wgrad, loss_sum = lax.psum((wgrad, loss_part), ('blk', 'rep'))]
    all_gather x1 -> x0, waiting for transfers between devices: 64.1 us -> none  [shards(): every_tok = lax.all_gather(ptok, 'blk', axis=0, tiled=True)]
    all_to_all x0 -> x4, blocking collectives: none -> 58.9 us  [the longest x1 23.1 us: shards(): part = lax.all_to_all(send, 'rep', 0, 0)]
    unnamed x23 -> x12, local copies, waits for them, and re-layouts: 33.8 us -> 5.32 us
    dot_general x7 -> x0, matrix products: 19.4 us -> none  [the longest x1 4.73 us: shards(): qgrad = jnp.dot(grad_a, every_tok, preferred_element_type=jnp.float32)]
    pallas_call x0 -> x5, Pallas kernels: none -> 17.8 us  [the longest x1 9.01 us: shards(): pl.pallas_call(functools.partial(score_kernel, qlen), name='scores', grid...]
  transfers between devices with their start and end apart: 3 -> 1, of which waited for: 3 -> 1; matrix products, arithmetic and copies ran while one was open for 2% -> 0% of each run, Pallas kernels for 0% -> 0%
where the time goes in v1:
time: 99.1 us; the launch traced here: 98.5 us
  blocking collectives  58.9 us (59%)
  Pallas kernels  17.8 us (18%)
  waiting for transfers between devices  7.58 us (8%)
  starting transfers between devices  7.48 us (8%)
  local copies, waits for them, and re-layouts  5.32 us (5%)
    all_to_all x1, blocking collectives, shards(): part = lax.all_to_all(send, 'rep', 0, 0)  23.1 us
    all_to_all x1, blocking collectives, shards(): wgrad = lax.all_to_all(part, 'rep', 0, 0).astype(F32).reshape(hidden, dim)  15.4 us
    all_to_all x1, blocking collectives, shards(): recv = lax.all_to_all(send, 'blk', 0, 0)  10.7 us
    all_to_all x1, blocking collectives, shards(): part = lax.all_to_all(part, 'blk', 0, 0)  9.68 us
    pallas_call x1, Pallas kernels, shards(): pl.pallas_call(functools.partial(score_kernel, qlen), name='scores', grid...  9.01 us
    all_to_all x1, waiting for transfers between devices, shards(): qt = lax.all_to_all(copies, 'blk', 0, 0)  7.58 us
    all_to_all x1, starting transfers between devices, shards(): qt = lax.all_to_all(copies, 'blk', 0, 0)  7.48 us
    pallas_call x1, Pallas kernels, shards(): pl.pallas_call(functools.partial(grad_kernel, qlen, float(total)), name='...  7.26 us
  transfers between devices with their start and end apart: 1, of which 1 were waited for; matrix products, arithmetic and copies ran while one was open for 0% of the time, Pallas kernels for 0%

profile of v1, /device:TPU:1, one launch (start us, length us, event | category | flops | bytes accessed | tf_op | source)
XLA Modules:
  0.0 98.5 jit_solution(7773248544630586805)
XLA Ops:
  0.6 0.0 copy-start.1
  0.6 0.9 copy-done.1
  1.6 0.0 copy-start.3
  1.6 0.9 copy-done.3
  2.5 0.0 copy-start.4
  2.5 1.0 query_tokens.1
  3.5 7.5 %all-to-all-start = ((bf16[8,128,128]{2,1,0:T(8,128)(2,1)}), bf16[8,128,128]{2,1,0:T(8,128)(2,1)S(1)}, u32[]{:S(2)}, u32[]{:S(2)}) async-start(bf16[8,128,128]{2,1,0:T(8,128)(2,1)} %query_tokens.1), calls=%async_computation | async-start | bytes 524288 | tf_op jit(solution)/shard_map/all_to_all | solution.py:215
  10.9 7.6 %all-to-all-done.qt_ref = bf16[8,128,128]{2,1,0:T(8,128)(2,1)S(1)} async-done(((bf16[8,128,128]{2,1,0:T(8,128)(2,1)}), bf16[8,128,128]{2,1,0:T(8,128)(2,1)S(1)}, u32[]{:S(2)}, u32[]{:S(2)}) %all-to-all-start) | async-done | bytes 262176 | tf_op jit(solution)/shard_map/all_to_all | solution.py:215
  18.5 0.0 copy-start
  18.5 1.9 %copy-done = bf16[1,4,512,768]{3,2,1,0:T(8,128)(2,1)S(1)} copy-done((bf16[1,4,512,768]{3,2,1,0:T(8,128)(2,1)S(1)}, bf16[1,4,512,768]{3,2,1,0:T(8,128)(2,1)}, u32[]{:S(2)}) %copy-start) | copy-done | bytes 3145752
  20.4 0.0 copy-start.2
  20.4 0.9 copy-done.2
  21.3 0.0 copy-start.5
  21.3 0.7 copy-done.5
  22.0 9.0 %scores.1 = (bf16[4,512,1024]{2,1,0:T(8,128)(2,1)}, f32[2,4,8,128]{3,2,1,0:T(8,128)S(1)}, bf16[8,160,128]{2,1,0:T(8,128)(2,1)S(1)}, f32[4,128,128]{2,1,0:T(8,128)S(1)}) custom-call(s32[4]{0:T(128)S(1)} %bitcast.15, s32[1]{0:T(128)} %bitcast.1.me_ref, bf16[8,128,128]{2,1,0:T(8,128)(2,1)S(1)} %all-to-all-done.qt_ref, bf16[4,512,768]{2,1,0:T(8,128)(2,1)S(1)} %bitcast.11, ...), custom_call_target="tpu_custom_call" | custom-call | tf_op jit(solution)/shard_map/scores/pallas_call | solution.py:217
  31.0 10.7 %all_to_all.25.recv_ref = bf16[8,160,128]{2,1,0:T(8,128)(2,1)S(1)} all-to-all(bf16[8,160,128]{2,1,0:T(8,128)(2,1)S(1)} %get-tuple-element.13), channel_id=1, replica_groups=mesh['blk'=8,'rep'=32] {'blk'}, dimensions={0} | all-to-all | bytes 655360 | tf_op jit(solution)/shard_map/all_to_all | solution.py:243
  41.7 0.0 copy-done.4
  41.7 7.3 %grads.1 = (f32[128,128]{1,0:T(8,128)}, f32[4,512,128]{2,1,0:T(8,128)}, bf16[32,32,128]{2,1,0:T(8,128)(2,1)S(1)}) custom-call(s32[4]{0:T(128)S(1)} %bitcast.16, s32[1]{0:T(128)} %bitcast.1.me_ref, bf16[8,160,128]{2,1,0:T(8,128)(2,1)S(1)} %all_to_all.25.recv_ref, bf16[4,512,1024]{2,1,0:T(8,128)(2,1)} %get-tuple-element.14.e_ref, ...), custom_call_target="tpu_custom_call" | custom-call | tf_op jit(solution)/shard_map/grads/pallas_call | solution.py:246
  49.0 23.1 %all_to_all.26.x_ref = bf16[32,32,128]{2,1,0:T(8,128)(2,1)S(1)} all-to-all(bf16[32,32,128]{2,1,0:T(8,128)(2,1)S(1)} %get-tuple-element.19), channel_id=1, replica_groups=mesh['blk'=8,'rep'=32] {'rep'}, dimensions={0} | all-to-all | bytes 524288 | tf_op jit(solution)/shard_map/all_to_all | solution.py:279
  72.1 0.1 sum_rep.1
  72.1 9.7 %all_to_all.27.x_ref = f32[8,32,128]{2,1,0:T(8,128)S(1)} all-to-all(f32[8,32,128]{2,1,0:T(8,128)S(1)} %sum_rep.1), channel_id=1, replica_groups=mesh['blk'=8,'rep'=32] {'blk'}, dimensions={0} | all-to-all | bytes 262144 | tf_op jit(solution)/shard_map/all_to_all | solution.py:288
  81.8 0.5 sum_blk.1
  82.3 15.4 %all_to_all.28 = bf16[32,24,128]{2,1,0:T(8,128)(2,1)S(1)} all-to-all(bf16[32,24,128]{2,1,0:T(8,128)(2,1)S(1)} %get-tuple-element.20), channel_id=1, replica_groups=mesh['blk'=8,'rep'=32] {'rep'}, dimensions={0} | all-to-all | bytes 393216 | tf_op jit(solution)/shard_map/all_to_all | solution.py:297
  97.8 0.8 bitcast_convert_fusion
Async XLA Ops:
  0.6 0.9 copy-start.1
  1.6 0.9 copy-start.3
  2.5 39.2 %copy-start.4 = (bf16[1,4,32,768]{3,2,1,0:T(8,128)(2,1)S(1)}, bf16[1,4,32,768]{3,2,1,0:T(8,128)(2,1)}, u32[]{:S(2)}) copy-start(bf16[1,4,32,768]{3,2,1,0:T(8,128)(2,1)} %param.4) | copy-start | bytes 589828
  3.5 15.1 %all-to-all-start = ((bf16[8,128,128]{2,1,0:T(8,128)(2,1)}), bf16[8,128,128]{2,1,0:T(8,128)(2,1)S(1)}, u32[]{:S(2)}, u32[]{:S(2)}) async-start(bf16[8,128,128]{2,1,0:T(8,128)(2,1)} %query_tokens.1), calls=%async_computation | async-start | bytes 524288 | tf_op jit(solution)/shard_map/all_to_all | solution.py:215
  18.5 1.9 %copy-start = (bf16[1,4,512,768]{3,2,1,0:T(8,128)(2,1)S(1)}, bf16[1,4,512,768]{3,2,1,0:T(8,128)(2,1)}, u32[]{:S(2)}) copy-start(bf16[1,4,512,768]{3,2,1,0:T(8,128)(2,1)} %param.5) | copy-start | bytes 9437188
  20.4 0.9 copy-start.2
  21.3 0.7 copy-start.5

commit v2 on v0

v2 whole, which is shorter than its diff:
```python
import functools
import math

import jax
import jax.numpy as jnp
from jax import lax
from jax.experimental import pallas as pl
from jax.experimental.pallas import tpu as pltpu
from jax.sharding import Mesh
from jax.sharding import PartitionSpec as P

F32 = jnp.float32
BF16 = jnp.bfloat16
INV_TEMPER = 2.0
TEMPER = 0.5
EXP2_SCALE = INV_TEMPER * math.log2(math.e)
LANES = 128
EXTRA = 32
AXES = ("x_hi", "y", "z", "x_lo", "core")
BLK = ("x_hi", "y")
REP = ("z", "x_lo", "core")
PLANE = ("x_hi", "y", "x_lo")
COLUMN = ("z", "core")
NN = (((1,), (0,)), ((), ()))
NT = (((1,), (1,)), ((), ()))
TN = (((0,), (0,)), ((), ()))


def mm(a, b, dims):
    return lax.dot_general(a, b, dims, preferred_element_type=F32)


def to_row(x):
    return jnp.concatenate([x[c : c + 1, :] for c in range(x.shape[0])], axis=1)


def to_chunks(x):
    n = x.shape[1] // LANES
    return jnp.concatenate([x[:, c * LANES : (c + 1) * LANES] for c in range(n)], axis=0)


def split3(x):
    hi = x.astype(BF16).astype(F32)
    rest = x - hi
    mid = rest.astype(BF16).astype(F32)
    return hi, mid, (rest - mid)


def segment_sum(x, width):
    lane = lax.broadcasted_iota(jnp.int32, x.shape, 1)
    step = 1
    while step < width:
        up = pltpu.roll(x, x.shape[1] - step, 1)
        down = pltpu.roll(x, step, 1)
        x = x + jnp.where((lane & step) == 0, up, down)
        step *= 2
    return x


def query_kernel(q_hbm, w_hbm, out_ref, q_ref, w_ref, sem):
    copies = [pltpu.make_async_copy(q_hbm, q_ref, sem.at[0]), pltpu.make_async_copy(w_hbm, w_ref, sem.at[1])]
    for copy in copies:
        copy.start()
    for copy in copies:
        copy.wait()
    tok = mm(q_ref[...], w_ref[...], NN)
    flipped = tok.T.astype(BF16)
    for c in range(out_ref.shape[0]):
        out_ref[c] = flipped


def passage_kernel(len_ref, me_ref, phid_hbm, w_hbm, tok_ref, tab_ref, phid_ref, w_ref, sem):
    npass = phid_ref.shape[0]
    copies = [pltpu.make_async_copy(w_hbm, w_ref, sem.at[npass])]
    copies += [pltpu.make_async_copy(phid_hbm.at[p], phid_ref.at[p], sem.at[p]) for p in range(npass)]
    for copy in copies:
        copy.start()
    shape = tab_ref.shape[1:]
    for p in range(npass):
        tab_ref[p] = jnp.full(shape, len_ref[p], jnp.int32)
    tab_ref[npass] = jnp.full(shape, me_ref[0], jnp.int32)
    copies[0].wait()
    for p in range(npass):
        copies[p + 1].wait()
        tok = mm(phid_ref[p], w_ref[...], NN)
        tok_ref[p, 0] = tok.astype(BF16)
        for r in range(0, tok.shape[0], LANES):
            tok_ref[p, 1, r : r + LANES, :] = tok[r : r + LANES, :].T.astype(BF16)


def score_kernel(qlen, qt_ref, tok_ref, tab_ref, e_ref, stat_ref, send_ref, own_ref, qs_ref, s_ref, g_ref):
    nblk = qt_ref.shape[0]
    npass, slots, ntok = e_ref.shape
    for c in range(nblk):
        qs_ref[:, c * LANES : (c + 1) * LANES] = qt_ref[c]
    rows = 128

    def fold(x, op):
        return functools.reduce(op, [x[r : r + 8] for r in range(0, x.shape[0], 8)])

    def scores(p):
        top = None
        count = tab_ref[p, :1, :1]
        for r in range(0, slots, rows):
            x = mm(tok_ref[p, 0, r : r + rows, :], qs_ref[...], NN)
            row = lax.broadcasted_iota(jnp.int32, (rows, 1), 0) + r
            x = jnp.where(row < count, x, -jnp.inf)
            s_ref[p % 2, r : r + rows, :] = x
            high = fold(x, jnp.maximum)
            top = high if top is None else jnp.maximum(top, high)
        return jnp.max(top, axis=0, keepdims=True)

    def powers(p, top):
        total = jnp.zeros((8, ntok), F32)
        for r in range(0, slots, 16):
            e = jnp.exp2((s_ref[p % 2, r : r + 16, :] - top) * EXP2_SCALE)
            total = total + fold(e, jnp.add)
            e_ref[p, r : r + 16, :] = e.astype(BF16)
        return jnp.sum(total, axis=0, keepdims=True)

    def finish(p, top, total):
        inv = 1.0 / total
        flipped = jnp.concatenate([tok_ref[p, 1, r : r + LANES, :] for r in range(0, slots, LANES)], axis=1)
        g = mm(flipped, e_ref[p], NN) * inv
        for c in range(nblk):
            g_ref[p, c] = g[:, c * LANES : (c + 1) * LANES]
        logz = to_chunks(top * INV_TEMPER + jnp.log(total))
        log_count = jnp.log(tab_ref[p].astype(F32))
        stat_ref[0, p] = segment_sum(TEMPER * (logz - log_count), qlen)
        stat_ref[1, p] = to_chunks(inv)

    top = scores(0)
    for p in range(npass):
        after = scores(p + 1) if p + 1 < npass else None
        total = powers(p, top)
        finish(p, top, total)
        top = after

    score = [stat_ref[0, k] for k in range(npass)]
    high = functools.reduce(jnp.maximum, score)
    lse = high + jnp.log(sum(jnp.exp(s - high) for s in score))
    share = [jnp.exp(s - lse) for s in score]
    hi, mid, lo = split3(lse)
    extra = jnp.concatenate([hi, mid, lo, jnp.zeros_like(lo)], axis=0).astype(BF16)
    me = tab_ref[npass, :1, :1]
    own = [jnp.zeros(own_ref.shape[1:], F32) for _ in range(npass)]
    for c in range(nblk):
        part = jnp.zeros(own_ref.shape[1:], F32)
        for k in range(npass):
            g = g_ref[k, c]
            part = part + g * share[k][c : c + 1, :]
            own[k] = jnp.where(me == c, g, own[k])
        send_ref[c, :LANES, :] = part.astype(BF16)
        send_ref[c, LANES:, :] = extra
    for k in range(npass):
        own_ref[k] = own[k]


def grad_kernel(
    qlen, total, tab_ref, recv_ref, e_ref, stat_ref, own_ref, qt_ref, phid_hbm, qhid_hbm,
    qgrad_ref, pgrad_ref, send_ref, acc_ref, qs_ref, phid_ref, qhid_ref, sem,
):
    nblk = qt_ref.shape[0]
    npass = stat_ref.shape[1]
    copies = [pltpu.make_async_copy(phid_hbm.at[p], phid_ref.at[p], sem.at[p]) for p in range(npass)]
    copies.append(pltpu.make_async_copy(qhid_hbm, qhid_ref, sem.at[npass]))
    for copy in copies:
        copy.start()
    me = tab_ref[npass, :1, :1]
    lane = lax.broadcasted_iota(jnp.int32, (nblk, LANES), 1)
    chunk = lax.broadcasted_iota(jnp.int32, (nblk, LANES), 0)
    mine = chunk == me

    def pick(x):
        return jnp.sum(jnp.where(mine, x, 0.0), axis=0, keepdims=True)

    parts = []
    for d in range(nblk):
        x = recv_ref[d, LANES:, :].astype(F32)
        parts.append(x[:nblk] + x[nblk : 2 * nblk] + x[2 * nblk : 3 * nblk])
    high = functools.reduce(jnp.maximum, parts)
    lse = high + jnp.log(sum(jnp.exp(x - high) for x in parts))
    dscore = []
    loss = jnp.zeros((nblk, LANES), F32)
    for k in range(npass):
        hit = mine & (lane // qlen == k)
        dscore.append((jnp.exp(stat_ref[0, k] - lse) - hit.astype(F32)) / total)
        loss = loss + jnp.where(mine & (lane == k * qlen), lse - stat_ref[0, k], 0.0)

    for p in range(npass):
        weight = dscore[p] * stat_ref[1, p]
        for c in range(nblk):
            qs_ref[p % 2, :, c * LANES : (c + 1) * LANES] = (
                qt_ref[c].astype(F32) * weight[c : c + 1, :]
            ).astype(BF16)
        pgrad = mm(e_ref[p], qs_ref[p % 2], NT)
        pgrad_ref[p] = pgrad
        copies[p].wait()
        term = mm(pgrad.astype(BF16), phid_ref[p], TN)
        if p == 0:
            acc_ref[...] = term
        else:
            acc_ref[...] += term

    grad = jnp.zeros((LANES, LANES), F32)
    for k in range(npass):
        grad = grad + own_ref[k] * pick(dscore[k])
    for d in range(nblk):
        share = jnp.where(me == d, 0.0, pick(jnp.exp(parts[d] - lse)) / total)
        grad = grad + recv_ref[d, :LANES, :].astype(F32) * share
    qgrad_ref[...] = grad.T
    copies[npass].wait()
    wgrad = (acc_ref[...] + mm(grad.astype(BF16), qhid_ref[...], NN)).T

    hi, mid, lo = split3(jnp.full((1, LANES), jnp.sum(loss)))
    extra = jnp.concatenate([hi, mid, lo, jnp.zeros((5, LANES), F32)], axis=0)
    rows = send_ref.shape[1] - 8
    for r in range(send_ref.shape[0]):
        send_ref[r] = jnp.concatenate([wgrad[r * rows : (r + 1) * rows, :], extra], axis=0).astype(BF16)


def sum_spread_kernel(x_ref, out_ref):
    y = jnp.sum(x_ref[...].astype(F32), axis=0)
    rows = y.shape[0] - 8
    hi, mid, lo = split3(jnp.sum(y[rows:], axis=0, keepdims=True))
    y = jnp.concatenate([y[:rows], hi, mid, lo, jnp.zeros((5, LANES), F32)], axis=0).astype(BF16)
    for c in range(out_ref.shape[0]):
        out_ref[c] = y


def sum_final_kernel(total, x_ref, out_ref, loss_ref):
    y = jnp.sum(x_ref[...].astype(F32), axis=0)
    rows = out_ref.shape[1]
    z = y[:rows].astype(BF16)
    for c in range(out_ref.shape[0]):
        out_ref[c] = z
    loss_ref[...] = jnp.sum(y[rows:], axis=0, keepdims=True) / total


def widen_kernel(x_ref, out_ref):
    rows = x_ref.shape[1]
    for c in range(x_ref.shape[0]):
        out_ref[c * rows : (c + 1) * rows, :] = x_ref[c].astype(F32)


VM = pl.BlockSpec(memory_space=pltpu.VMEM)
SM = pl.BlockSpec(memory_space=pltpu.SMEM)
HBM = pl.BlockSpec(memory_space=pltpu.HBM)


def call(name, kernel, ins, out_shape, *args, scratch=(), flops=0, bytes_accessed=0):
    args = [pltpu.with_memory_space_constraint(a, pltpu.HBM) if i is HBM else a for a, i in zip(args, ins)]
    return pl.pallas_call(
        kernel,
        name=name,
        out_shape=out_shape,
        in_specs=ins,
        out_specs=jax.tree.map(lambda _: VM, out_shape),
        scratch_shapes=scratch,
        compiler_params=pltpu.CompilerParams(vmem_limit_bytes=32 << 20),
        cost_estimate=pl.CostEstimate(flops=flops, bytes_accessed=bytes_accessed, transcendentals=0),
    )(*args)


def shards(query_hidden, passage_hidden, lengths, projection):
    hidden, dim = projection.shape
    nquery, qlen = query_hidden.shape[1:3]
    npass, plen = passage_hidden.shape[1:3]
    nblk, nrep = lax.axis_size(BLK), lax.axis_size(REP)
    nplane, ncolumn = lax.axis_size(PLANE), lax.axis_size(COLUMN)
    total = nblk * nrep * nquery
    mine = nquery * qlen
    ntok = nblk * mine
    rows = hidden // nplane
    qflat = query_hidden[0].reshape(-1, hidden)
    me = lax.axis_index(BLK).astype(jnp.int32)[None]
    S = jax.ShapeDtypeStruct

    copies = call(
        "query_tokens", query_kernel, [HBM, HBM], S((nblk, dim, mine), BF16), qflat, projection,
        scratch=[pltpu.VMEM((mine, hidden), BF16), pltpu.VMEM((hidden, dim), BF16), pltpu.SemaphoreType.DMA((2,))],
        flops=2 * mine * hidden * dim, bytes_accessed=400_000,
    )
    qt = lax.all_to_all(copies, BLK, 0, 0)
    tok, tab = call(
        "passage_tokens", passage_kernel, [SM, SM, HBM, HBM],
        (S((npass, 2, plen, dim), BF16), S((npass + 1, nblk, LANES), jnp.int32)),
        lengths[0], me, passage_hidden[0], projection,
        scratch=[pltpu.VMEM((npass, plen, hidden), BF16), pltpu.VMEM((hidden, dim), BF16),
                 pltpu.SemaphoreType.DMA((npass + 1,))],
        flops=2 * npass * plen * hidden * dim, bytes_accessed=8_000_000,
    )
    e, stat, send, own = call(
        "scores", functools.partial(score_kernel, qlen), [VM] * 3,
        (S((npass, plen, ntok), BF16), S((2, npass, nblk, LANES), F32), S((nblk, dim + EXTRA, LANES), BF16),
         S((npass, dim, LANES), F32)),
        qt, tok, tab,
        scratch=[pltpu.VMEM((dim, ntok), BF16), pltpu.VMEM((2, plen, ntok), F32),
                 pltpu.VMEM((npass, nblk, dim, LANES), F32)],
        flops=4 * npass * plen * ntok * dim, bytes_accessed=8_000_000,
    )
    recv = lax.all_to_all(send, BLK, 0, 0)
    qgrad, pgrad, send = call(
        "grads", functools.partial(grad_kernel, qlen, float(total)), [VM] * 6 + [HBM] * 2,
        (S((mine, dim), F32), S((npass, plen, dim), F32), S((nplane, rows + 8, dim), BF16)),
        tab, recv, e, stat, own, qt, passage_hidden[0], qflat,
        scratch=[pltpu.VMEM((dim, hidden), F32), pltpu.VMEM((2, dim, ntok), BF16), pltpu.VMEM((npass, plen, hidden), BF16),
                 pltpu.VMEM((mine, hidden), BF16), pltpu.SemaphoreType.DMA((npass + 1,))],
        flops=2 * npass * plen * ntok * dim, bytes_accessed=8_000_000,
    )
    part = lax.all_to_all(send, PLANE, 0, 0)
    part = call("sum_plane", sum_spread_kernel, [VM], S((ncolumn, rows + 8, dim), BF16), part)
    part = lax.all_to_all(part, COLUMN, 0, 0)
    part, loss = call(
        "sum_column", functools.partial(sum_final_kernel, float(total)), [VM],
        (S((nplane, rows, dim), BF16), S((1, dim), F32)), part,
    )
    wgrad = call("widen", widen_kernel, [VM], S((hidden, dim), F32), lax.all_to_all(part, PLANE, 0, 0))
    return (
        qgrad.reshape(1, nquery, qlen, dim),
        pgrad.reshape(1, npass, plen, dim),
        wgrad,
        loss[0, 0],
    )


def solution(mesh):
    fine = Mesh(mesh.devices.reshape(2, 4, 8, 2, 2), AXES)
    return jax.shard_map(
        shards,
        mesh=fine,
        in_specs=(P(REP, BLK, None, None), P(REP, BLK, None, None), P(REP, BLK), P()),
        out_specs=(P(REP, BLK, None, None), P(REP, BLK, None, None), P(), P()),
        check_vma=False,
    )
```

time: 522 us -> 84.2 us (0.16)
  waiting for transfers between devices: 352 us -> 2.59 us
  local copies, waits for them, and re-layouts: 35.5 us -> 0.65 us
  blocking collectives: 86.2 us -> 55.8 us
  matrix products: 19.4 us -> 0 us
  Pallas kernels: 0 us -> 16.6 us
  between operations: 16.4 us -> 0.67 us
  other arithmetic: 11.2 us -> 0 us
  starting transfers between devices: 0.12 us -> 7.49 us
    psum x1 -> x0, waiting for transfers between devices: 175 us -> none  [shards(): wgrad, loss_sum = lax.psum((wgrad, loss_part), ('blk', 'rep'))]
    reduce_scatter x1 -> x0, waiting for transfers between devices: 113 us -> none  [shards(): lax.psum_scatter(jnp.dot(grad_a.T, qtok, preferred_element_type=jnp.float...]
    psum x1 -> x0, blocking collectives: 74.6 us -> none  [shards(): wgrad, loss_sum = lax.psum((wgrad, loss_part), ('blk', 'rep'))]
    all_gather x1 -> x0, waiting for transfers between devices: 64.1 us -> none  [shards(): every_tok = lax.all_gather(ptok, 'blk', axis=0, tiled=True)]
    all_to_all x0 -> x4, blocking collectives: none -> 55.8 us  [the longest x1 23.1 us: shards(): part = lax.all_to_all(part, COLUMN, 0, 0)]
    unnamed x23 -> x2, local copies, waits for them, and re-layouts: 33.8 us -> 0.65 us
    dot_general x7 -> x0, matrix products: 19.4 us -> none  [the longest x1 4.73 us: shards(): qgrad = jnp.dot(grad_a, every_tok, preferred_element_type=jnp.float32)]
    pallas_call x0 -> x7, Pallas kernels: none -> 16.6 us  [call(): pl.pallas_call(kernel, name=name, out_shape=out_shape, in_specs=ins, out_...]
  transfers between devices with their start and end apart: 3 -> 1, of which waited for: 3 -> 1; matrix products, arithmetic and copies ran while one was open for 2% -> 0% of each run, Pallas kernels for 0% -> 5%
where the time goes in v2:
time: 84.2 us; the launch traced here: 83.8 us
  blocking collectives  55.8 us (66%)
  Pallas kernels  16.6 us (20%)
  starting transfers between devices  7.49 us (9%)
  waiting for transfers between devices  2.59 us (3%)
    all_to_all x1, blocking collectives, shards(): part = lax.all_to_all(part, COLUMN, 0, 0)  23.1 us
    pallas_call x7, Pallas kernels, call(): pl.pallas_call(kernel, name=name, out_shape=out_shape, in_specs=ins, out_...  16.6 us
    all_to_all x1, blocking collectives, shards(): recv = lax.all_to_all(send, BLK, 0, 0)  12 us
    all_to_all x1, blocking collectives, shards(): lax.all_to_all(part, PLANE, 0, 0)  10.7 us
    all_to_all x1, blocking collectives, shards(): part = lax.all_to_all(send, PLANE, 0, 0)  9.97 us
    all_to_all x1, starting transfers between devices, shards(): qt = lax.all_to_all(copies, BLK, 0, 0)  7.49 us
    all_to_all x1, waiting for transfers between devices, shards(): qt = lax.all_to_all(copies, BLK, 0, 0)  2.59 us
  transfers between devices with their start and end apart: 1, of which 1 were waited for; matrix products, arithmetic and copies ran while one was open for 0% of the time, Pallas kernels for 5%

profile of v2, /device:TPU:1, one launch (start us, length us, event | category | flops | bytes accessed | tf_op | source)
XLA Modules:
  0.0 83.8 jit_solution(13118026528334244668)
XLA Ops:
  0.6 2.0 %query_tokens.1 = bf16[8,128,128]{2,1,0:T(8,128)(2,1)} custom-call(bf16[128,768]{1,0:T(8,128)(2,1)} %bitcast.11, bf16[768,128]{1,0:T(8,128)(2,1)} %w_hbm.3), custom_call_target="tpu_custom_call" | custom-call | flops 25165824 | bytes 400000 | tf_op jit(solution)/shard_map/query_tokens/pallas_call | solution.py:253
  2.6 7.5 %all-to-all-start = ((bf16[8,128,128]{2,1,0:T(8,128)(2,1)}), bf16[8,128,128]{2,1,0:T(8,128)(2,1)S(1)}, u32[]{:S(2)}, u32[]{:S(2)}) async-start(bf16[8,128,128]{2,1,0:T(8,128)(2,1)} %query_tokens.1), calls=%async_computation | async-start | bytes 524288 | tf_op jit(solution)/shard_map/all_to_all | solution.py:284
  10.1 0.0 copy-start
  10.1 0.7 copy-done
  10.8 4.3 %passage_tokens.1 = (bf16[4,2,512,128]{3,2,1,0:T(8,128)(2,1)S(1)}, s32[5,8,128]{2,1,0:T(8,128)S(1)}) custom-call(s32[4]{0:T(128)S(1)} %bitcast.8, s32[1]{0:T(128)} %bitcast.1.me_ref, bf16[4,512,768]{2,1,0:T(8,128)(2,1)} %bitcast.9, bf16[768,128]{1,0:T(8,128)(2,1)} %w_hbm.3), custom_call_target="tpu_custom_call" | custom-call | flops 402653184 | bytes 8000000 | tf_op jit(solution)/shard_map/passage_tokens/pallas_call | solution.py:253
  15.1 2.6 %all-to-all-done.qt_ref = bf16[8,128,128]{2,1,0:T(8,128)(2,1)S(1)} async-done(((bf16[8,128,128]{2,1,0:T(8,128)(2,1)}), bf16[8,128,128]{2,1,0:T(8,128)(2,1)S(1)}, u32[]{:S(2)}, u32[]{:S(2)}) %all-to-all-start) | async-done | bytes 262176 | tf_op jit(solution)/shard_map/all_to_all | solution.py:284
  17.7 4.0 %scores.1 = (bf16[4,512,1024]{2,1,0:T(8,128)(2,1)S(1)}, f32[2,4,8,128]{3,2,1,0:T(8,128)S(1)}, bf16[8,160,128]{2,1,0:T(8,128)(2,1)S(1)}, f32[4,128,128]{2,1,0:T(8,128)S(1)}) custom-call(bf16[8,128,128]{2,1,0:T(8,128)(2,1)S(1)} %all-to-all-done.qt_ref, bf16[4,2,512,128]{3,2,1,0:T(8,128)(2,1)S(1)} %get-tuple-element.16.tok_ref, ...), custom_call_target="tpu_custom_call" | custom-call | flops 1073741824 | bytes 8000000 | tf_op jit(solution)/shard_map/scores/pallas_call | solution.py:253
  21.7 12.0 %all_to_all.25.recv_ref = bf16[8,160,128]{2,1,0:T(8,128)(2,1)S(1)} all-to-all(bf16[8,160,128]{2,1,0:T(8,128)(2,1)S(1)} %get-tuple-element.17), channel_id=1, replica_groups=mesh['x_hi'=2,'y'=4,'z'=8,'x_lo'=2,'core'=2] {'x_hi','y'}, dimensions={0} | all-to-all | bytes 655360 | tf_op jit(solution)/shard_map/all_to_all | solution.py:302
  33.7 4.9 %grads.1 = (f32[128,128]{1,0:T(8,128)}, f32[4,512,128]{2,1,0:T(8,128)}, bf16[16,56,128]{2,1,0:T(8,128)(2,1)S(1)}) custom-call(s32[5,8,128]{2,1,0:T(8,128)S(1)} %get-tuple-element.15.tab_ref, bf16[8,160,128]{2,1,0:T(8,128)(2,1)S(1)} %all_to_all.25.recv_ref, bf16[4,512,1024]{2,1,0:T(8,128)(2,1)S(1)} %get-tuple-element.18.e_ref, ...), custom_call_target="tpu_custom_call" | custom-call | flops 536870912 | bytes 8000000 | tf_op jit(solution)/shard_map/grads/pallas_call | solution.py:253
  38.6 10.0 %all_to_all.26.x_ref = bf16[16,56,128]{2,1,0:T(8,128)(2,1)S(1)} all-to-all(bf16[16,56,128]{2,1,0:T(8,128)(2,1)S(1)} %get-tuple-element.23), channel_id=1, replica_groups=mesh['x_hi'=2,'y'=4,'z'=8,'x_lo'=2,'core'=2] {'x_hi','y','x_lo'}, dimensions={0} | all-to-all | bytes 458752 | tf_op jit(solution)/shard_map/all_to_all | solution.py:311
  48.6 23.1 %all_to_all.27.x_ref = bf16[16,56,128]{2,1,0:T(8,128)(2,1)S(1)} all-to-all(bf16[16,56,128]{2,1,0:T(8,128)(2,1)S(1)} %sum_plane.1), channel_id=1, replica_groups=mesh['x_hi'=2,'y'=4,'z'=8,'x_lo'=2,'core'=2] {'z','core'}, dimensions={0} | all-to-all | bytes 458752 | tf_op jit(solution)/shard_map/all_to_all | solution.py:313
  71.7 0.6 sum_column.1
  72.3 10.7 %all_to_all.28.x_ref = bf16[16,48,128]{2,1,0:T(8,128)(2,1)S(1)} all-to-all(bf16[16,48,128]{2,1,0:T(8,128)(2,1)S(1)} %get-tuple-element.24), channel_id=1, replica_groups=mesh['x_hi'=2,'y'=4,'z'=8,'x_lo'=2,'core'=2] {'x_hi','y','x_lo'}, dimensions={0} | all-to-all | bytes 393216 | tf_op jit(solution)/shard_map/all_to_all | solution.py:318
  83.0 0.8 widen.1
  (1 shorter events, 0.0 us)
Async XLA Ops:
  2.6 15.1 %all-to-all-start = ((bf16[8,128,128]{2,1,0:T(8,128)(2,1)}), bf16[8,128,128]{2,1,0:T(8,128)(2,1)S(1)}, u32[]{:S(2)}, u32[]{:S(2)}) async-start(bf16[8,128,128]{2,1,0:T(8,128)(2,1)} %query_tokens.1), calls=%async_computation | async-start | bytes 524288 | tf_op jit(solution)/shard_map/all_to_all | solution.py:284
  10.1 0.7 copy-start

commit v3 on v2

--- a/solution.py
+++ b/solution.py
@@ -15,12 +15,12 @@
 TEMPER = 0.5
 EXP2_SCALE = INV_TEMPER * math.log2(math.e)
 LANES = 128
-EXTRA = 32
+EXTRA = 8
 AXES = ("x_hi", "y", "z", "x_lo", "core")
 BLK = ("x_hi", "y")
 REP = ("z", "x_lo", "core")
-PLANE = ("x_hi", "y", "x_lo")
-COLUMN = ("z", "core")
+PLANE = ("x_hi", "y", "x_lo", "core")
+COLUMN = "z"
 NN = (((1,), (0,)), ((), ()))
 NT = (((1,), (1,)), ((), ()))
 TN = (((0,), (0,)), ((), ()))
@@ -69,16 +69,19 @@
         out_ref[c] = flipped
 
 
-def passage_kernel(len_ref, me_ref, phid_hbm, w_hbm, tok_ref, tab_ref, phid_ref, w_ref, sem):
+def passage_kernel(len_hbm, phid_hbm, w_hbm, tok_ref, tab_ref, phid_ref, w_ref, len_ref, sem):
     npass = phid_ref.shape[0]
+    lens = pltpu.make_async_copy(len_hbm, len_ref, sem.at[npass + 1])
+    lens.start()
     copies = [pltpu.make_async_copy(w_hbm, w_ref, sem.at[npass])]
     copies += [pltpu.make_async_copy(phid_hbm.at[p], phid_ref.at[p], sem.at[p]) for p in range(npass)]
     for copy in copies:
         copy.start()
     shape = tab_ref.shape[1:]
+    tab_ref[npass] = jnp.full(shape, lax.axis_index("x_hi") * lax.axis_size("y") + lax.axis_index("y"), jnp.int32)
+    lens.wait()
     for p in range(npass):
-        tab_ref[p] = jnp.full(shape, len_ref[p], jnp.int32)
-    tab_ref[npass] = jnp.full(shape, me_ref[0], jnp.int32)
+        tab_ref[p] = jnp.full(shape, len_ref[0, p], jnp.int32)
     copies[0].wait()
     for p in range(npass):
         copies[p + 1].wait()
@@ -141,7 +144,8 @@
     lse = high + jnp.log(sum(jnp.exp(s - high) for s in score))
     share = [jnp.exp(s - lse) for s in score]
     hi, mid, lo = split3(lse)
-    extra = jnp.concatenate([hi, mid, lo, jnp.zeros_like(lo)], axis=0).astype(BF16)
+    place = lax.broadcasted_iota(jnp.int32, lse.shape, 1) % qlen
+    extra = jnp.where(place == 0, hi, jnp.where(place == 1, mid, lo)).astype(BF16)
     me = tab_ref[npass, :1, :1]
     own = [jnp.zeros(own_ref.shape[1:], F32) for _ in range(npass)]
     for c in range(nblk):
@@ -158,7 +162,7 @@
 
 def grad_kernel(
     qlen, total, tab_ref, recv_ref, e_ref, stat_ref, own_ref, qt_ref, phid_hbm, qhid_hbm,
-    qgrad_ref, pgrad_ref, send_ref, acc_ref, qs_ref, phid_ref, qhid_ref, sem,
+    qgrad_hbm, pgrad_hbm, send_ref, acc_ref, qs_ref, phid_ref, qhid_ref, qgrad_ref, pgrad_ref, sem, out_sem,
 ):
     nblk = qt_ref.shape[0]
     npass = stat_ref.shape[1]
@@ -177,7 +181,7 @@
     parts = []
     for d in range(nblk):
         x = recv_ref[d, LANES:, :].astype(F32)
-        parts.append(x[:nblk] + x[nblk : 2 * nblk] + x[2 * nblk : 3 * nblk])
+        parts.append(segment_sum(jnp.where(lane % qlen < 3, x, 0.0), qlen))
     high = functools.reduce(jnp.maximum, parts)
     lse = high + jnp.log(sum(jnp.exp(x - high) for x in parts))
     dscore = []
@@ -187,6 +191,19 @@
         dscore.append((jnp.exp(stat_ref[0, k] - lse) - hit.astype(F32)) / total)
         loss = loss + jnp.where(mine & (lane == k * qlen), lse - stat_ref[0, k], 0.0)
 
+    grad = jnp.zeros((LANES, LANES), F32)
+    for k in range(npass):
+        grad = grad + own_ref[k] * pick(dscore[k])
+    for d in range(nblk):
+        share = jnp.where(me == d, 0.0, pick(jnp.exp(parts[d] - lse)) / total)
+        grad = grad + recv_ref[d, :LANES, :].astype(F32) * share
+    qgrad_ref[...] = grad.T
+    outs = [pltpu.make_async_copy(qgrad_ref, qgrad_hbm, out_sem.at[npass])]
+    outs[0].start()
+    copies[npass].wait()
+    acc_ref[...] = mm(grad.astype(BF16), qhid_ref[...], NN)
+
+
     for p in range(npass):
         weight = dscore[p] * stat_ref[1, p]
         for c in range(nblk):
@@ -195,67 +212,55 @@
             ).astype(BF16)
         pgrad = mm(e_ref[p], qs_ref[p % 2], NT)
         pgrad_ref[p] = pgrad
+        outs.append(pltpu.make_async_copy(pgrad_ref.at[p], pgrad_hbm.at[p], out_sem.at[p]))
+        outs[-1].start()
         copies[p].wait()
-        term = mm(pgrad.astype(BF16), phid_ref[p], TN)
-        if p == 0:
-            acc_ref[...] = term
-        else:
-            acc_ref[...] += term
-
-    grad = jnp.zeros((LANES, LANES), F32)
-    for k in range(npass):
-        grad = grad + own_ref[k] * pick(dscore[k])
-    for d in range(nblk):
-        share = jnp.where(me == d, 0.0, pick(jnp.exp(parts[d] - lse)) / total)
-        grad = grad + recv_ref[d, :LANES, :].astype(F32) * share
-    qgrad_ref[...] = grad.T
-    copies[npass].wait()
-    wgrad = (acc_ref[...] + mm(grad.astype(BF16), qhid_ref[...], NN)).T
+        acc_ref[...] += mm(pgrad.astype(BF16), phid_ref[p], TN)
+    wgrad = acc_ref[...].T
 
     hi, mid, lo = split3(jnp.full((1, LANES), jnp.sum(loss)))
     extra = jnp.concatenate([hi, mid, lo, jnp.zeros((5, LANES), F32)], axis=0)
     rows = send_ref.shape[1] - 8
     for r in range(send_ref.shape[0]):
         send_ref[r] = jnp.concatenate([wgrad[r * rows : (r + 1) * rows, :], extra], axis=0).astype(BF16)
-
-
-def sum_spread_kernel(x_ref, out_ref):
+    for copy in outs:
+        copy.wait()
+
+
+def sum_plane_kernel(x_ref, out_ref):
     y = jnp.sum(x_ref[...].astype(F32), axis=0)
-    rows = y.shape[0] - 8
-    hi, mid, lo = split3(jnp.sum(y[rows:], axis=0, keepdims=True))
-    y = jnp.concatenate([y[:rows], hi, mid, lo, jnp.zeros((5, LANES), F32)], axis=0).astype(BF16)
     for c in range(out_ref.shape[0]):
         out_ref[c] = y
 
 
-def sum_final_kernel(total, x_ref, out_ref, loss_ref):
-    y = jnp.sum(x_ref[...].astype(F32), axis=0)
+def sum_column_kernel(total, x_ref, out_ref, loss_ref):
+    y = jnp.sum(x_ref[...], axis=0)
     rows = out_ref.shape[1]
     z = y[:rows].astype(BF16)
     for c in range(out_ref.shape[0]):
         out_ref[c] = z
-    loss_ref[...] = jnp.sum(y[rows:], axis=0, keepdims=True) / total
-
-
-def widen_kernel(x_ref, out_ref):
+    loss_ref[...] = jnp.broadcast_to(jnp.sum(y[rows:], axis=0, keepdims=True) / total, loss_ref.shape)
+
+
+def final_kernel(x_ref, loss_in_ref, out_ref, loss_ref):
     rows = x_ref.shape[1]
+    loss_ref[...] = loss_in_ref[:1, :]
     for c in range(x_ref.shape[0]):
         out_ref[c * rows : (c + 1) * rows, :] = x_ref[c].astype(F32)
 
 
 VM = pl.BlockSpec(memory_space=pltpu.VMEM)
-SM = pl.BlockSpec(memory_space=pltpu.SMEM)
 HBM = pl.BlockSpec(memory_space=pltpu.HBM)
 
 
-def call(name, kernel, ins, out_shape, *args, scratch=(), flops=0, bytes_accessed=0):
+def call(name, kernel, ins, out_shape, *args, outs=None, scratch=(), flops=0, bytes_accessed=0):
     args = [pltpu.with_memory_space_constraint(a, pltpu.HBM) if i is HBM else a for a, i in zip(args, ins)]
     return pl.pallas_call(
         kernel,
         name=name,
         out_shape=out_shape,
         in_specs=ins,
-        out_specs=jax.tree.map(lambda _: VM, out_shape),
+        out_specs=outs or jax.tree.map(lambda _: VM, out_shape),
         scratch_shapes=scratch,
         compiler_params=pltpu.CompilerParams(vmem_limit_bytes=32 << 20),
         cost_estimate=pl.CostEstimate(flops=flops, bytes_accessed=bytes_accessed, transcendentals=0),
@@ -273,7 +278,6 @@
     ntok = nblk * mine
     rows = hidden // nplane
     qflat = query_hidden[0].reshape(-1, hidden)
-    me = lax.axis_index(BLK).astype(jnp.int32)[None]
     S = jax.ShapeDtypeStruct
 
     copies = call(
@@ -283,11 +287,11 @@
     )
     qt = lax.all_to_all(copies, BLK, 0, 0)
     tok, tab = call(
-        "passage_tokens", passage_kernel, [SM, SM, HBM, HBM],
+        "passage_tokens", passage_kernel, [HBM, HBM, HBM],
         (S((npass, 2, plen, dim), BF16), S((npass + 1, nblk, LANES), jnp.int32)),
-        lengths[0], me, passage_hidden[0], projection,
+        lengths, passage_hidden[0], projection,
         scratch=[pltpu.VMEM((npass, plen, hidden), BF16), pltpu.VMEM((hidden, dim), BF16),
-                 pltpu.SemaphoreType.DMA((npass + 1,))],
+                 pltpu.SMEM(lengths.shape, jnp.int32), pltpu.SemaphoreType.DMA((npass + 2,))],
         flops=2 * npass * plen * hidden * dim, bytes_accessed=8_000_000,
     )
     e, stat, send, own = call(
@@ -305,17 +309,20 @@
         (S((mine, dim), F32), S((npass, plen, dim), F32), S((nplane, rows + 8, dim), BF16)),
         tab, recv, e, stat, own, qt, passage_hidden[0], qflat,
         scratch=[pltpu.VMEM((dim, hidden), F32), pltpu.VMEM((2, dim, ntok), BF16), pltpu.VMEM((npass, plen, hidden), BF16),
-                 pltpu.VMEM((mine, hidden), BF16), pltpu.SemaphoreType.DMA((npass + 1,))],
+                 pltpu.VMEM((mine, hidden), BF16), pltpu.VMEM((mine, dim), F32), pltpu.VMEM((npass, plen, dim), F32),
+                 pltpu.SemaphoreType.DMA((npass + 1,)), pltpu.SemaphoreType.DMA((npass + 1,))],
+        outs=(HBM, HBM, VM),
         flops=2 * npass * plen * ntok * dim, bytes_accessed=8_000_000,
     )
     part = lax.all_to_all(send, PLANE, 0, 0)
-    part = call("sum_plane", sum_spread_kernel, [VM], S((ncolumn, rows + 8, dim), BF16), part)
+    part = call("sum_plane", sum_plane_kernel, [VM], S((ncolumn, rows + 8, dim), F32), part)
     part = lax.all_to_all(part, COLUMN, 0, 0)
     part, loss = call(
-        "sum_column", functools.partial(sum_final_kernel, float(total)), [VM],
-        (S((nplane, rows, dim), BF16), S((1, dim), F32)), part,
-    )
-    wgrad = call("widen", widen_kernel, [VM], S((hidden, dim), F32), lax.all_to_all(part, PLANE, 0, 0))
+        "sum_column", functools.partial(sum_column_kernel, float(total)), [VM],
+        (S((nplane, rows, dim), BF16), S((8, dim), F32)), part,
+    )
+    part = lax.all_to_all(part, PLANE, 0, 0)
+    wgrad, loss = call("final", final_kernel, [VM, VM], (S((hidden, dim), F32), S((1, dim), F32)), part, loss)
     return (
         qgrad.reshape(1, nquery, qlen, dim),
         pgrad.reshape(1, npass, plen, dim),

time: 84.2 us -> 84 us (level)
  blocking collectives: 55.8 us -> 54.6 us
  waiting for transfers between devices: 2.59 us -> 3.77 us
    all_to_all x1, blocking collectives: 23.1 us -> 16 us  [shards(): part = lax.all_to_all(part, COLUMN, 0, 0)]
    all_to_all x1, blocking collectives: 9.97 us -> 14.5 us  [shards(): part = lax.all_to_all(send, PLANE, 0, 0)]
    all_to_all x1, blocking collectives: 10.7 us -> 13.4 us  [shards(): part = lax.all_to_all(part, PLANE, 0, 0)]
    all_to_all x1, blocking collectives: 12 us -> 10.7 us  [shards(): recv = lax.all_to_all(send, BLK, 0, 0)]
    all_to_all x1, waiting for transfers between devices: 2.59 us -> 3.77 us  [shards(): qt = lax.all_to_all(copies, BLK, 0, 0)]
where the time goes in v3:
time: 84 us; the launch traced here: 83.6 us
  blocking collectives  54.6 us (65%)
  Pallas kernels  17.1 us (20%)
  starting transfers between devices  7.49 us (9%)
  waiting for transfers between devices  3.77 us (4%)
    pallas_call x7, Pallas kernels, call(): pl.pallas_call(kernel, name=name, out_shape=out_shape, in_specs=ins, out_...  17.1 us
    all_to_all x1, blocking collectives, shards(): part = lax.all_to_all(part, COLUMN, 0, 0)  16 us
    all_to_all x1, blocking collectives, shards(): part = lax.all_to_all(send, PLANE, 0, 0)  14.5 us
    all_to_all x1, blocking collectives, shards(): part = lax.all_to_all(part, PLANE, 0, 0)  13.4 us
    all_to_all x1, blocking collectives, shards(): recv = lax.all_to_all(send, BLK, 0, 0)  10.7 us
    all_to_all x1, starting transfers between devices, shards(): qt = lax.all_to_all(copies, BLK, 0, 0)  7.49 us
    all_to_all x1, waiting for transfers between devices, shards(): qt = lax.all_to_all(copies, BLK, 0, 0)  3.77 us
  transfers between devices with their start and end apart: 1, of which 1 were waited for; matrix products, arithmetic and copies ran while one was open for 0% of the time, Pallas kernels for 5%

profile of v3, /device:TPU:1, one launch (start us, length us, event | category | flops | bytes accessed | tf_op | source)
XLA Modules:
  0.0 83.6 jit_solution(4928689419285555358)
XLA Ops:
  0.6 2.0 %query_tokens.1 = bf16[8,128,128]{2,1,0:T(8,128)(2,1)} custom-call(bf16[128,768]{1,0:T(8,128)(2,1)} %bitcast.8, bf16[768,128]{1,0:T(8,128)(2,1)} %w_hbm.3), custom_call_target="tpu_custom_call" | custom-call | flops 25165824 | bytes 400000 | tf_op jit(solution)/shard_map/query_tokens/pallas_call | solution.py:258
  2.6 7.5 %all-to-all-start = ((bf16[8,128,128]{2,1,0:T(8,128)(2,1)}), bf16[8,128,128]{2,1,0:T(8,128)(2,1)S(1)}, u32[]{:S(2)}, u32[]{:S(2)}) async-start(bf16[8,128,128]{2,1,0:T(8,128)(2,1)} %query_tokens.1), calls=%async_computation | async-start | bytes 524288 | tf_op jit(solution)/shard_map/all_to_all | solution.py:288
  10.1 3.8 %passage_tokens.1 = (bf16[4,2,512,128]{3,2,1,0:T(8,128)(2,1)S(1)}, s32[5,8,128]{2,1,0:T(8,128)S(1)}) custom-call(s32[1,4]{1,0:T(1,128)} %len_hbm.1, bf16[4,512,768]{2,1,0:T(8,128)(2,1)} %bitcast.6, bf16[768,128]{1,0:T(8,128)(2,1)} %w_hbm.3), custom_call_target="tpu_custom_call" | custom-call | flops 402653184 | bytes 8000000 | tf_op jit(solution)/shard_map/passage_tokens/pallas_call | solution.py:258
  13.9 3.8 %all-to-all-done.qt_ref = bf16[8,128,128]{2,1,0:T(8,128)(2,1)S(1)} async-done(((bf16[8,128,128]{2,1,0:T(8,128)(2,1)}), bf16[8,128,128]{2,1,0:T(8,128)(2,1)S(1)}, u32[]{:S(2)}, u32[]{:S(2)}) %all-to-all-start) | async-done | bytes 262176 | tf_op jit(solution)/shard_map/all_to_all | solution.py:288
  17.7 4.0 %scores.1 = (bf16[4,512,1024]{2,1,0:T(8,128)(2,1)S(1)}, f32[2,4,8,128]{3,2,1,0:T(8,128)S(1)}, bf16[8,136,128]{2,1,0:T(8,128)(2,1)S(1)}, f32[4,128,128]{2,1,0:T(8,128)S(1)}) custom-call(bf16[8,128,128]{2,1,0:T(8,128)(2,1)S(1)} %all-to-all-done.qt_ref, bf16[4,2,512,128]{3,2,1,0:T(8,128)(2,1)S(1)} %get-tuple-element.18.tok_ref, ...), custom_call_target="tpu_custom_call" | custom-call | flops 1073741824 | bytes 8000000 | tf_op jit(solution)/shard_map/scores/pallas_call | solution.py:258
  21.7 10.7 %all_to_all.25.recv_ref = bf16[8,136,128]{2,1,0:T(8,128)(2,1)S(1)} all-to-all(bf16[8,136,128]{2,1,0:T(8,128)(2,1)S(1)} %get-tuple-element.19), channel_id=1, replica_groups=mesh['x_hi'=2,'y'=4,'z'=8,'x_lo'=2,'core'=2] {'x_hi','y'}, dimensions={0} | all-to-all | bytes 557056 | tf_op jit(solution)/shard_map/all_to_all | solution.py:306
  32.4 6.4 %grads.1 = (f32[128,128]{1,0:T(8,128)}, f32[4,512,128]{2,1,0:T(8,128)}, bf16[32,32,128]{2,1,0:T(8,128)(2,1)S(1)}) custom-call(s32[5,8,128]{2,1,0:T(8,128)S(1)} %get-tuple-element.17.tab_ref, bf16[8,136,128]{2,1,0:T(8,128)(2,1)S(1)} %all_to_all.25.recv_ref, bf16[4,512,1024]{2,1,0:T(8,128)(2,1)S(1)} %get-tuple-element.20.e_ref, ...), custom_call_target="tpu_custom_call" | custom-call | flops 536870912 | bytes 8000000 | tf_op jit(solution)/shard_map/grads/pallas_call | solution.py:258
  38.8 14.5 %all_to_all.26.x_ref = bf16[32,32,128]{2,1,0:T(8,128)(2,1)S(1)} all-to-all(bf16[32,32,128]{2,1,0:T(8,128)(2,1)S(1)} %get-tuple-element.25), channel_id=1, replica_groups=mesh['x_hi'=2,'y'=4,'z'=8,'x_lo'=2,'core'=2] {'x_hi','y','x_lo','core'}, dimensions={0} | all-to-all | bytes 524288 | tf_op jit(solution)/shard_map/all_to_all | solution.py:317
  53.3 0.1 sum_plane.1
  53.3 16.0 %all_to_all.27.x_ref = f32[8,32,128]{2,1,0:T(8,128)S(1)} all-to-all(f32[8,32,128]{2,1,0:T(8,128)S(1)} %sum_plane.1), channel_id=1, replica_groups=mesh['x_hi'=2,'y'=4,'z'=8,'x_lo'=2,'core'=2] {'z'}, dimensions={0} | all-to-all | bytes 262144 | tf_op jit(solution)/shard_map/all_to_all | solution.py:319
  69.4 13.4 %all_to_all.28.x_ref = bf16[32,24,128]{2,1,0:T(8,128)(2,1)S(1)} all-to-all(bf16[32,24,128]{2,1,0:T(8,128)(2,1)S(1)} %get-tuple-element.26), channel_id=1, replica_groups=mesh['x_hi'=2,'y'=4,'z'=8,'x_lo'=2,'core'=2] {'x_hi','y','x_lo','core'}, dimensions={0} | all-to-all | bytes 393216 | tf_op jit(solution)/shard_map/all_to_all | solution.py:324
  82.8 0.8 final.1
  (1 shorter events, 0.0 us)
Async XLA Ops:
  2.6 15.1 %all-to-all-start = ((bf16[8,128,128]{2,1,0:T(8,128)(2,1)}), bf16[8,128,128]{2,1,0:T(8,128)(2,1)S(1)}, u32[]{:S(2)}, u32[]{:S(2)}) async-start(bf16[8,128,128]{2,1,0:T(8,128)(2,1)} %query_tokens.1), calls=%async_computation | async-start | bytes 524288 | tf_op jit(solution)/shard_map/all_to_all | solution.py:288

commit v4 on v3

--- a/solution.py
+++ b/solution.py
@@ -57,12 +57,7 @@
     return x
 
 
-def query_kernel(q_hbm, w_hbm, out_ref, q_ref, w_ref, sem):
-    copies = [pltpu.make_async_copy(q_hbm, q_ref, sem.at[0]), pltpu.make_async_copy(w_hbm, w_ref, sem.at[1])]
-    for copy in copies:
-        copy.start()
-    for copy in copies:
-        copy.wait()
+def query_kernel(q_ref, w_ref, out_ref):
     tok = mm(q_ref[...], w_ref[...], NN)
     flipped = tok.T.astype(BF16)
     for c in range(out_ref.shape[0]):
@@ -74,7 +69,7 @@
     lens = pltpu.make_async_copy(len_hbm, len_ref, sem.at[npass + 1])
     lens.start()
     copies = [pltpu.make_async_copy(w_hbm, w_ref, sem.at[npass])]
-    copies += [pltpu.make_async_copy(phid_hbm.at[p], phid_ref.at[p], sem.at[p]) for p in range(npass)]
+    copies += [pltpu.make_async_copy(phid_hbm, phid_ref, sem.at[0])]
     for copy in copies:
         copy.start()
     shape = tab_ref.shape[1:]
@@ -83,15 +78,23 @@
     for p in range(npass):
         tab_ref[p] = jnp.full(shape, len_ref[0, p], jnp.int32)
     copies[0].wait()
+    copies[1].wait()
     for p in range(npass):
-        copies[p + 1].wait()
         tok = mm(phid_ref[p], w_ref[...], NN)
         tok_ref[p, 0] = tok.astype(BF16)
         for r in range(0, tok.shape[0], LANES):
             tok_ref[p, 1, r : r + LANES, :] = tok[r : r + LANES, :].T.astype(BF16)
 
 
-def score_kernel(qlen, qt_ref, tok_ref, tab_ref, e_ref, stat_ref, send_ref, own_ref, qs_ref, s_ref, g_ref):
+def score_kernel(
+    qlen, qt_ref, tok_ref, tab_ref, phid_hbm, e_ref, stat_ref, send_ref, own_ref, phid_ref,
+    qs_ref, s_ref, g_ref, sem,
+):
+    copies = [
+        pltpu.make_async_copy(phid_hbm, phid_ref, sem.at[0]),
+    ]
+    for copy in copies:
+        copy.start()
     nblk = qt_ref.shape[0]
     npass, slots, ntok = e_ref.shape
     for c in range(nblk):
@@ -144,8 +147,8 @@
     lse = high + jnp.log(sum(jnp.exp(s - high) for s in score))
     share = [jnp.exp(s - lse) for s in score]
     hi, mid, lo = split3(lse)
-    place = lax.broadcasted_iota(jnp.int32, lse.shape, 1) % qlen
-    extra = jnp.where(place == 0, hi, jnp.where(place == 1, mid, lo)).astype(BF16)
+    place = lax.broadcasted_iota(jnp.int32, lse.shape, 1) % 4
+    extra = jnp.where(place == 0, hi, jnp.where(place == 1, mid, jnp.where(place == 2, lo, 0.0))).astype(BF16)
     me = tab_ref[npass, :1, :1]
     own = [jnp.zeros(own_ref.shape[1:], F32) for _ in range(npass)]
     for c in range(nblk):
@@ -158,18 +161,16 @@
         send_ref[c, LANES:, :] = extra
     for k in range(npass):
         own_ref[k] = own[k]
+    for copy in copies:
+        copy.wait()
 
 
 def grad_kernel(
-    qlen, total, tab_ref, recv_ref, e_ref, stat_ref, own_ref, qt_ref, phid_hbm, qhid_hbm,
-    qgrad_hbm, pgrad_hbm, send_ref, acc_ref, qs_ref, phid_ref, qhid_ref, qgrad_ref, pgrad_ref, sem, out_sem,
+    qlen, total, tab_ref, recv_ref, e_ref, stat_ref, own_ref, qt_ref, phid_ref, qhid_ref,
+    qgrad_ref, pgrad_ref, send_ref, acc_ref, qs_ref,
 ):
     nblk = qt_ref.shape[0]
     npass = stat_ref.shape[1]
-    copies = [pltpu.make_async_copy(phid_hbm.at[p], phid_ref.at[p], sem.at[p]) for p in range(npass)]
-    copies.append(pltpu.make_async_copy(qhid_hbm, qhid_ref, sem.at[npass]))
-    for copy in copies:
-        copy.start()
     me = tab_ref[npass, :1, :1]
     lane = lax.broadcasted_iota(jnp.int32, (nblk, LANES), 1)
     chunk = lax.broadcasted_iota(jnp.int32, (nblk, LANES), 0)
@@ -180,8 +181,7 @@
 
     parts = []
     for d in range(nblk):
-        x = recv_ref[d, LANES:, :].astype(F32)
-        parts.append(segment_sum(jnp.where(lane % qlen < 3, x, 0.0), qlen))
+        parts.append(segment_sum(recv_ref[d, LANES:, :].astype(F32), 4))
     high = functools.reduce(jnp.maximum, parts)
     lse = high + jnp.log(sum(jnp.exp(x - high) for x in parts))
     dscore = []
@@ -191,19 +191,6 @@
         dscore.append((jnp.exp(stat_ref[0, k] - lse) - hit.astype(F32)) / total)
         loss = loss + jnp.where(mine & (lane == k * qlen), lse - stat_ref[0, k], 0.0)
 
-    grad = jnp.zeros((LANES, LANES), F32)
-    for k in range(npass):
-        grad = grad + own_ref[k] * pick(dscore[k])
-    for d in range(nblk):
-        share = jnp.where(me == d, 0.0, pick(jnp.exp(parts[d] - lse)) / total)
-        grad = grad + recv_ref[d, :LANES, :].astype(F32) * share
-    qgrad_ref[...] = grad.T
-    outs = [pltpu.make_async_copy(qgrad_ref, qgrad_hbm, out_sem.at[npass])]
-    outs[0].start()
-    copies[npass].wait()
-    acc_ref[...] = mm(grad.astype(BF16), qhid_ref[...], NN)
-
-
     for p in range(npass):
         weight = dscore[p] * stat_ref[1, p]
         for c in range(nblk):
@@ -212,19 +199,23 @@
             ).astype(BF16)
         pgrad = mm(e_ref[p], qs_ref[p % 2], NT)
         pgrad_ref[p] = pgrad
-        outs.append(pltpu.make_async_copy(pgrad_ref.at[p], pgrad_hbm.at[p], out_sem.at[p]))
-        outs[-1].start()
-        copies[p].wait()
-        acc_ref[...] += mm(pgrad.astype(BF16), phid_ref[p], TN)
-    wgrad = acc_ref[...].T
+        term = mm(pgrad.astype(BF16), phid_ref[p], TN)
+        acc_ref[...] = term if p == 0 else acc_ref[...] + term
+    grad = jnp.zeros((LANES, LANES), F32)
+    for k in range(npass):
+        grad = grad + own_ref[k] * pick(dscore[k])
+    for d in range(nblk):
+        share = jnp.where(me == d, 0.0, pick(jnp.exp(parts[d] - lse)) / total)
+        grad = grad + recv_ref[d, :LANES, :].astype(F32) * share
+    qgrad_ref[...] = grad.T
+    wgrad = (acc_ref[...] + mm(grad.astype(BF16), qhid_ref[...], NN)).T
+
 
     hi, mid, lo = split3(jnp.full((1, LANES), jnp.sum(loss)))
     extra = jnp.concatenate([hi, mid, lo, jnp.zeros((5, LANES), F32)], axis=0)
     rows = send_ref.shape[1] - 8
     for r in range(send_ref.shape[0]):
         send_ref[r] = jnp.concatenate([wgrad[r * rows : (r + 1) * rows, :], extra], axis=0).astype(BF16)
-    for copy in outs:
-        copy.wait()
 
 
 def sum_plane_kernel(x_ref, out_ref):
@@ -251,10 +242,11 @@
 
 VM = pl.BlockSpec(memory_space=pltpu.VMEM)
 HBM = pl.BlockSpec(memory_space=pltpu.HBM)
+FAR = pl.BlockSpec(memory_space=pltpu.VMEM)
 
 
 def call(name, kernel, ins, out_shape, *args, outs=None, scratch=(), flops=0, bytes_accessed=0):
-    args = [pltpu.with_memory_space_constraint(a, pltpu.HBM) if i is HBM else a for a, i in zip(args, ins)]
+    args = [pltpu.with_memory_space_constraint(a, pltpu.HBM) if i is HBM or i is FAR else a for a, i in zip(args, ins)]
     return pl.pallas_call(
         kernel,
         name=name,
@@ -265,6 +257,60 @@
         compiler_params=pltpu.CompilerParams(vmem_limit_bytes=32 << 20),
         cost_estimate=pl.CostEstimate(flops=flops, bytes_accessed=bytes_accessed, transcendentals=0),
     )(*args)
+
+
+def query_call(qhid, projection, nblk):
+    mine, hidden = qhid.shape
+    dim = projection.shape[1]
+    return call(
+        "query_tokens", query_kernel, [FAR, FAR], pltpu.VMEM((nblk, dim, mine), BF16), qhid, projection,
+        flops=2 * mine * hidden * dim, bytes_accessed=400_000,
+    )
+
+
+def passage_call(lengths, phid, projection, nblk):
+    npass, plen, hidden = phid.shape
+    dim = projection.shape[1]
+    S = jax.ShapeDtypeStruct
+    return call(
+        "passage_tokens", passage_kernel, [HBM, HBM, HBM],
+        (S((npass, 2, plen, dim), BF16), S((npass + 1, nblk, LANES), jnp.int32)),
+        lengths, phid, projection,
+        scratch=[pltpu.VMEM((npass, plen, hidden), BF16), pltpu.VMEM((hidden, dim), BF16),
+                 pltpu.SMEM(lengths.shape, jnp.int32), pltpu.SemaphoreType.DMA((npass + 2,))],
+        flops=2 * npass * plen * hidden * dim, bytes_accessed=8_000_000,
+    )
+
+
+def score_call(qt, tok, tab, phid, qlen):
+    nblk, dim, _ = qt.shape
+    npass, _, plen, _ = tok.shape
+    ntok = nblk * LANES
+    S = jax.ShapeDtypeStruct
+    return call(
+        "scores", functools.partial(score_kernel, qlen), [VM] * 3 + [HBM],
+        (S((npass, plen, ntok), BF16), S((2, npass, nblk, LANES), F32), S((nblk, dim + EXTRA, LANES), BF16),
+         S((npass, dim, LANES), F32), S(phid.shape, BF16)),
+        qt, tok, tab, phid,
+        scratch=[pltpu.VMEM((dim, ntok), BF16), pltpu.VMEM((2, plen, ntok), F32),
+                 pltpu.VMEM((npass, nblk, dim, LANES), F32), pltpu.SemaphoreType.DMA((2,))],
+        flops=4 * npass * plen * ntok * dim, bytes_accessed=8_000_000,
+    )
+
+
+def grad_call(tab, recv, e, stat, own, qt, phid, qhid, qlen, total, nplane):
+    npass, plen, ntok = e.shape
+    mine, hidden = qhid.shape
+    dim = qt.shape[1]
+    rows = hidden // nplane
+    S = jax.ShapeDtypeStruct
+    return call(
+        "grads", functools.partial(grad_kernel, qlen, total), [VM] * 8,
+        (S((mine, dim), F32), S((npass, plen, dim), F32), S((nplane, rows + 8, dim), BF16)),
+        tab, recv, e, stat, own, qt, phid, qhid,
+        scratch=[pltpu.VMEM((dim, hidden), F32), pltpu.VMEM((2, dim, ntok), BF16)],
+        flops=2 * npass * plen * ntok * dim, bytes_accessed=8_000_000,
+    )
 
 
 def shards(query_hidden, passage_hidden, lengths, projection):
@@ -280,40 +326,12 @@
     qflat = query_hidden[0].reshape(-1, hidden)
     S = jax.ShapeDtypeStruct
 
-    copies = call(
-        "query_tokens", query_kernel, [HBM, HBM], S((nblk, dim, mine), BF16), qflat, projection,
-        scratch=[pltpu.VMEM((mine, hidden), BF16), pltpu.VMEM((hidden, dim), BF16), pltpu.SemaphoreType.DMA((2,))],
-        flops=2 * mine * hidden * dim, bytes_accessed=400_000,
-    )
+    copies = query_call(qflat, projection, nblk)
     qt = lax.all_to_all(copies, BLK, 0, 0)
-    tok, tab = call(
-        "passage_tokens", passage_kernel, [HBM, HBM, HBM],
-        (S((npass, 2, plen, dim), BF16), S((npass + 1, nblk, LANES), jnp.int32)),
-        lengths, passage_hidden[0], projection,
-        scratch=[pltpu.VMEM((npass, plen, hidden), BF16), pltpu.VMEM((hidden, dim), BF16),
-                 pltpu.SMEM(lengths.shape, jnp.int32), pltpu.SemaphoreType.DMA((npass + 2,))],
-        flops=2 * npass * plen * hidden * dim, bytes_accessed=8_000_000,
-    )
-    e, stat, send, own = call(
-        "scores", functools.partial(score_kernel, qlen), [VM] * 3,
-        (S((npass, plen, ntok), BF16), S((2, npass, nblk, LANES), F32), S((nblk, dim + EXTRA, LANES), BF16),
-         S((npass, dim, LANES), F32)),
-        qt, tok, tab,
-        scratch=[pltpu.VMEM((dim, ntok), BF16), pltpu.VMEM((2, plen, ntok), F32),
-                 pltpu.VMEM((npass, nblk, dim, LANES), F32)],
-        flops=4 * npass * plen * ntok * dim, bytes_accessed=8_000_000,
-    )
+    tok, tab = passage_call(lengths, passage_hidden[0], projection, nblk)
+    e, stat, send, own, phid = score_call(qt, tok, tab, passage_hidden[0], qlen)
     recv = lax.all_to_all(send, BLK, 0, 0)
-    qgrad, pgrad, send = call(
-        "grads", functools.partial(grad_kernel, qlen, float(total)), [VM] * 6 + [HBM] * 2,
-        (S((mine, dim), F32), S((npass, plen, dim), F32), S((nplane, rows + 8, dim), BF16)),
-        tab, recv, e, stat, own, qt, passage_hidden[0], qflat,
-        scratch=[pltpu.VMEM((dim, hidden), F32), pltpu.VMEM((2, dim, ntok), BF16), pltpu.VMEM((npass, plen, hidden), BF16),
-                 pltpu.VMEM((mine, hidden), BF16), pltpu.VMEM((mine, dim), F32), pltpu.VMEM((npass, plen, dim), F32),
-                 pltpu.SemaphoreType.DMA((npass + 1,)), pltpu.SemaphoreType.DMA((npass + 1,))],
-        outs=(HBM, HBM, VM),
-        flops=2 * npass * plen * ntok * dim, bytes_accessed=8_000_000,
-    )
+    qgrad, pgrad, send = grad_call(tab, recv, e, stat, own, qt, phid, qflat, qlen, float(total), nplane)
     part = lax.all_to_all(send, PLANE, 0, 0)
     part = call("sum_plane", sum_plane_kernel, [VM], S((ncolumn, rows + 8, dim), F32), part)
     part = lax.all_to_all(part, COLUMN, 0, 0)

time: 84 us -> 80.7 us (0.961)
  Pallas kernels: 17.1 us -> 13.2 us
    pallas_call x7, Pallas kernels: 17.1 us -> 13.2 us  [call(): pl.pallas_call(kernel, name=name, out_shape=out_shape, in_specs=ins, out_...]
  transfers between devices with their start and end apart: 1 -> 1, of which waited for: 1 -> 1; matrix products, arithmetic and copies ran while one was open for 0% -> 0% of each run, Pallas kernels for 5% -> 4%
where the time goes in v4:
time: 80.7 us; the launch traced here: 80.3 us
  blocking collectives  54.6 us (68%)
  Pallas kernels  13.2 us (16%)
  starting transfers between devices  7.48 us (9%)
  waiting for transfers between devices  4.42 us (5%)
    all_to_all x1, blocking collectives, shards(): part = lax.all_to_all(part, COLUMN, 0, 0)  16 us
    all_to_all x1, blocking collectives, shards(): part = lax.all_to_all(send, PLANE, 0, 0)  14.5 us
    all_to_all x1, blocking collectives, shards(): part = lax.all_to_all(part, PLANE, 0, 0)  13.4 us
    pallas_call x7, Pallas kernels, call(): pl.pallas_call(kernel, name=name, out_shape=out_shape, in_specs=ins, out_...  13.2 us
    all_to_all x1, blocking collectives, shards(): recv = lax.all_to_all(send, BLK, 0, 0)  10.6 us
    all_to_all x1, starting transfers between devices, shards(): qt = lax.all_to_all(copies, BLK, 0, 0)  7.48 us
    all_to_all x1, waiting for transfers between devices, shards(): qt = lax.all_to_all(copies, BLK, 0, 0)  4.42 us
  transfers between devices with their start and end apart: 1, of which 1 were waited for; matrix products, arithmetic and copies ran while one was open for 0% of the time, Pallas kernels for 4%

profile of v4, /device:TPU:1, one launch (start us, length us, event | category | flops | bytes accessed | tf_op | source)
XLA Modules:
  0.0 80.3 jit_solution(632236642711023195)
XLA Ops:
  0.6 2.0 %query_tokens.1 = bf16[8,128,128]{2,1,0:T(8,128)(2,1)} custom-call(bf16[128,768]{1,0:T(8,128)(2,1)} %bitcast.6, bf16[768,128]{1,0:T(8,128)(2,1)} %w_ref.1), custom_call_target="tpu_custom_call" | custom-call | flops 25165824 | bytes 400000 | tf_op jit(solution)/shard_map/query_tokens/pallas_call | solution.py:250
  2.6 7.5 %all-to-all-start = ((bf16[8,128,128]{2,1,0:T(8,128)(2,1)}), bf16[8,128,128]{2,1,0:T(8,128)(2,1)S(1)}, u32[]{:S(2)}, u32[]{:S(2)}) async-start(bf16[8,128,128]{2,1,0:T(8,128)(2,1)} %query_tokens.1), calls=%async_computation | async-start | bytes 524288 | tf_op jit(solution)/shard_map/all_to_all | solution.py:330
  10.1 3.1 %passage_tokens.1 = (bf16[4,2,512,128]{3,2,1,0:T(8,128)(2,1)S(1)}, s32[5,8,128]{2,1,0:T(8,128)S(1)}) custom-call(s32[1,4]{1,0:T(1,128)} %len_hbm.1, bf16[4,512,768]{2,1,0:T(8,128)(2,1)} %bitcast.8, bf16[768,128]{1,0:T(8,128)(2,1)} %w_ref.1), custom_call_target="tpu_custom_call" | custom-call | flops 402653184 | bytes 8000000 | tf_op jit(solution)/shard_map/passage_tokens/pallas_call | solution.py:250
  13.3 0.0 copy-start
  13.3 4.4 %all-to-all-done.qt_ref = bf16[8,128,128]{2,1,0:T(8,128)(2,1)S(1)} async-done(((bf16[8,128,128]{2,1,0:T(8,128)(2,1)}), bf16[8,128,128]{2,1,0:T(8,128)(2,1)S(1)}, u32[]{:S(2)}, u32[]{:S(2)}) %all-to-all-start) | async-done | bytes 262176 | tf_op jit(solution)/shard_map/all_to_all | solution.py:330
  17.7 4.0 %scores.1 = (bf16[4,512,1024]{2,1,0:T(8,128)(2,1)S(1)}, f32[2,4,8,128]{3,2,1,0:T(8,128)S(1)}, bf16[8,136,128]{2,1,0:T(8,128)(2,1)S(1)}, f32[4,128,128]{2,1,0:T(8,128)S(1)}, bf16[4,512,768]{2,1,0:T(8,128)(2,1)S(1)}) custom-call(bf16[8,128,128]{2,1,0:T(8,128)(2,1)S(1)} %all-to-all-done.qt_ref, bf16[4,2,512,128]{3,2,1,0:T(8,128)(2,1)S(1)} %get-tuple-element.19.tok_ref, ...), custom_call_target="tpu_custom_call" | custom-call | flops 1073741824 | bytes 8000000 | tf_op jit(solution)/shard_map/scores/pallas_call | solution.py:250
  21.7 10.6 %all_to_all.25.recv_ref = bf16[8,136,128]{2,1,0:T(8,128)(2,1)S(1)} all-to-all(bf16[8,136,128]{2,1,0:T(8,128)(2,1)S(1)} %get-tuple-element.20), channel_id=1, replica_groups=mesh['x_hi'=2,'y'=4,'z'=8,'x_lo'=2,'core'=2] {'x_hi','y'}, dimensions={0} | all-to-all | bytes 557056 | tf_op jit(solution)/shard_map/all_to_all | solution.py:333
  32.3 0.0 copy-done
  32.3 3.2 %grads.1 = (f32[128,128]{1,0:T(8,128)}, f32[4,512,128]{2,1,0:T(8,128)}, bf16[32,32,128]{2,1,0:T(8,128)(2,1)S(1)}) custom-call(s32[5,8,128]{2,1,0:T(8,128)S(1)} %get-tuple-element.18.tab_ref, bf16[8,136,128]{2,1,0:T(8,128)(2,1)S(1)} %all_to_all.25.recv_ref, bf16[4,512,1024]{2,1,0:T(8,128)(2,1)S(1)} %get-tuple-element.21.e_ref, ...), custom_call_target="tpu_custom_call" | custom-call | flops 536870912 | bytes 8000000 | tf_op jit(solution)/shard_map/grads/pallas_call | solution.py:250
  35.5 14.5 %all_to_all.26.x_ref = bf16[32,32,128]{2,1,0:T(8,128)(2,1)S(1)} all-to-all(bf16[32,32,128]{2,1,0:T(8,128)(2,1)S(1)} %get-tuple-element.27), channel_id=1, replica_groups=mesh['x_hi'=2,'y'=4,'z'=8,'x_lo'=2,'core'=2] {'x_hi','y','x_lo','core'}, dimensions={0} | all-to-all | bytes 524288 | tf_op jit(solution)/shard_map/all_to_all | solution.py:335
  50.0 0.1 sum_plane.1
  50.0 16.0 %all_to_all.27.x_ref = f32[8,32,128]{2,1,0:T(8,128)S(1)} all-to-all(f32[8,32,128]{2,1,0:T(8,128)S(1)} %sum_plane.1), channel_id=1, replica_groups=mesh['x_hi'=2,'y'=4,'z'=8,'x_lo'=2,'core'=2] {'z'}, dimensions={0} | all-to-all | bytes 262144 | tf_op jit(solution)/shard_map/all_to_all | solution.py:337
  66.1 13.4 %all_to_all.28.x_ref = bf16[32,24,128]{2,1,0:T(8,128)(2,1)S(1)} all-to-all(bf16[32,24,128]{2,1,0:T(8,128)(2,1)S(1)} %get-tuple-element.28), channel_id=1, replica_groups=mesh['x_hi'=2,'y'=4,'z'=8,'x_lo'=2,'core'=2] {'x_hi','y','x_lo','core'}, dimensions={0} | all-to-all | bytes 393216 | tf_op jit(solution)/shard_map/all_to_all | solution.py:342
  79.5 0.8 final.1
  (1 shorter events, 0.0 us)
Async XLA Ops:
  2.6 15.1 %all-to-all-start = ((bf16[8,128,128]{2,1,0:T(8,128)(2,1)}), bf16[8,128,128]{2,1,0:T(8,128)(2,1)S(1)}, u32[]{:S(2)}, u32[]{:S(2)}) async-start(bf16[8,128,128]{2,1,0:T(8,128)(2,1)} %query_tokens.1), calls=%async_computation | async-start | bytes 524288 | tf_op jit(solution)/shard_map/all_to_all | solution.py:330
  13.3 19.0 %copy-start = (bf16[1,4,32,768]{3,2,1,0:T(8,128)(2,1)S(1)}, bf16[1,4,32,768]{3,2,1,0:T(8,128)(2,1)}, u32[]{:S(2)}) copy-start(bf16[1,4,32,768]{3,2,1,0:T(8,128)(2,1)} %param.4) | copy-start | bytes 589828

commit v5 on v4

--- a/solution.py
+++ b/solution.py
@@ -19,7 +19,7 @@
 AXES = ("x_hi", "y", "z", "x_lo", "core")
 BLK = ("x_hi", "y")
 REP = ("z", "x_lo", "core")
-PLANE = ("x_hi", "y", "x_lo", "core")
+PLANE = ("x_hi", "y", "x_lo")
 COLUMN = "z"
 NN = (((1,), (0,)), ((), ()))
 NT = (((1,), (1,)), ((), ()))
@@ -69,7 +69,9 @@
     lens = pltpu.make_async_copy(len_hbm, len_ref, sem.at[npass + 1])
     lens.start()
     copies = [pltpu.make_async_copy(w_hbm, w_ref, sem.at[npass])]
-    copies += [pltpu.make_async_copy(phid_hbm, phid_ref, sem.at[0])]
+    half = npass // 2
+    for k, at in enumerate((pl.ds(0, half), pl.ds(half, npass - half))):
+        copies.append(pltpu.make_async_copy(phid_hbm.at[at], phid_ref.at[at], sem.at[k]))
     for copy in copies:
         copy.start()
     shape = tab_ref.shape[1:]
@@ -78,8 +80,11 @@
     for p in range(npass):
         tab_ref[p] = jnp.full(shape, len_ref[0, p], jnp.int32)
     copies[0].wait()
-    copies[1].wait()
     for p in range(npass):
+        if p == 0:
+            copies[1].wait()
+        if p == half:
+            copies[2].wait()
         tok = mm(phid_ref[p], w_ref[...], NN)
         tok_ref[p, 0] = tok.astype(BF16)
         for r in range(0, tok.shape[0], LANES):
@@ -167,7 +172,7 @@
 
 def grad_kernel(
     qlen, total, tab_ref, recv_ref, e_ref, stat_ref, own_ref, qt_ref, phid_ref, qhid_ref,
-    qgrad_ref, pgrad_ref, send_ref, acc_ref, qs_ref,
+    qgrad_ref, pgrad_ref, send_ref, acc_ref, qs_ref, small_ref,
 ):
     nblk = qt_ref.shape[0]
     npass = stat_ref.shape[1]
@@ -199,8 +204,8 @@
             ).astype(BF16)
         pgrad = mm(e_ref[p], qs_ref[p % 2], NT)
         pgrad_ref[p] = pgrad
-        term = mm(pgrad.astype(BF16), phid_ref[p], TN)
-        acc_ref[...] = term if p == 0 else acc_ref[...] + term
+        small_ref[p * pgrad.shape[0] : (p + 1) * pgrad.shape[0], :] = pgrad.astype(BF16)
+    acc_ref[...] = mm(small_ref[...], phid_ref[...].reshape(small_ref.shape[0], -1), TN)
     grad = jnp.zeros((LANES, LANES), F32)
     for k in range(npass):
         grad = grad + own_ref[k] * pick(dscore[k])
@@ -219,13 +224,20 @@
 
 
 def sum_plane_kernel(x_ref, out_ref):
-    y = jnp.sum(x_ref[...].astype(F32), axis=0)
+    out_ref[...] = jnp.sum(x_ref[...].astype(F32), axis=0)
+
+
+def sum_pair_kernel(x_ref, y_ref, out_ref):
+    y = x_ref[...] + y_ref[...]
+    rows = y.shape[0] - 8
+    hi, mid, lo = split3(jnp.sum(y[rows:], axis=0, keepdims=True))
+    y = jnp.concatenate([y[:rows], hi, mid, lo, jnp.zeros((5, LANES), F32)], axis=0).astype(BF16)
     for c in range(out_ref.shape[0]):
         out_ref[c] = y
 
 
 def sum_column_kernel(total, x_ref, out_ref, loss_ref):
-    y = jnp.sum(x_ref[...], axis=0)
+    y = jnp.sum(x_ref[...].astype(F32), axis=0)
     rows = out_ref.shape[1]
     z = y[:rows].astype(BF16)
     for c in range(out_ref.shape[0]):
@@ -308,7 +320,7 @@
         "grads", functools.partial(grad_kernel, qlen, total), [VM] * 8,
         (S((mine, dim), F32), S((npass, plen, dim), F32), S((nplane, rows + 8, dim), BF16)),
         tab, recv, e, stat, own, qt, phid, qhid,
-        scratch=[pltpu.VMEM((dim, hidden), F32), pltpu.VMEM((2, dim, ntok), BF16)],
+        scratch=[pltpu.VMEM((dim, hidden), F32), pltpu.VMEM((2, dim, ntok), BF16), pltpu.VMEM((npass * plen, dim), BF16)],
         flops=2 * npass * plen * ntok * dim, bytes_accessed=8_000_000,
     )
 
@@ -333,7 +345,9 @@
     recv = lax.all_to_all(send, BLK, 0, 0)
     qgrad, pgrad, send = grad_call(tab, recv, e, stat, own, qt, phid, qflat, qlen, float(total), nplane)
     part = lax.all_to_all(send, PLANE, 0, 0)
-    part = call("sum_plane", sum_plane_kernel, [VM], S((ncolumn, rows + 8, dim), F32), part)
+    part = call("sum_plane", sum_plane_kernel, [VM], S((rows + 8, dim), F32), part)
+    twin = lax.ppermute(part, "core", [(0, 1), (1, 0)])
+    part = call("sum_pair", sum_pair_kernel, [VM, VM], S((ncolumn, rows + 8, dim), BF16), part, twin)
     part = lax.all_to_all(part, COLUMN, 0, 0)
     part, loss = call(
         "sum_column", functools.partial(sum_column_kernel, float(total)), [VM],

time: 80.7 us -> 78.4 us (0.971); the launches traced: 80.3 us -> 77 us
  blocking collectives: 54.6 us -> 46 us
  starting transfers between devices: 7.48 us -> 11.9 us
  waiting for transfers between devices: 4.42 us -> 5.48 us
    all_to_all x1, blocking collectives: 14.5 us -> 9.95 us  [shards(): part = lax.all_to_all(send, PLANE, 0, 0)]
    ppermute x0 -> x1, starting transfers between devices: none -> 4.47 us  [shards(): twin = lax.ppermute(part, 'core', [(0, 1), (1, 0)])]
    all_to_all x1, blocking collectives: 13.4 us -> 9.86 us  [shards(): part = lax.all_to_all(part, PLANE, 0, 0)]
    ppermute x0 -> x1, waiting for transfers between devices: none -> 0.85 us  [shards(): twin = lax.ppermute(part, 'core', [(0, 1), (1, 0)])]
    pallas_call x7 -> x8, Pallas kernels: 13.2 us -> 12.9 us  [call(): pl.pallas_call(kernel, name=name, out_shape=out_shape, in_specs=ins, out_...]
  transfers between devices with their start and end apart: 1 -> 2, of which waited for: 1 -> 2; matrix products, arithmetic and copies ran while one was open for 0% -> 0% of each run, Pallas kernels for 4% -> 4%
where the time goes in v5:
time: 78.4 us; the launch traced here: 77 us
  blocking collectives  46 us (59%)
  Pallas kernels  12.9 us (16%)
  starting transfers between devices  11.9 us (15%)
  waiting for transfers between devices  5.48 us (7%)
    all_to_all x1, blocking collectives, shards(): part = lax.all_to_all(part, COLUMN, 0, 0)  15.6 us
    pallas_call x8, Pallas kernels, call(): pl.pallas_call(kernel, name=name, out_shape=out_shape, in_specs=ins, out_...  12.9 us
    all_to_all x1, blocking collectives, shards(): recv = lax.all_to_all(send, BLK, 0, 0)  10.6 us
    all_to_all x1, blocking collectives, shards(): part = lax.all_to_all(send, PLANE, 0, 0)  9.95 us
    all_to_all x1, blocking collectives, shards(): part = lax.all_to_all(part, PLANE, 0, 0)  9.86 us
    all_to_all x1, starting transfers between devices, shards(): qt = lax.all_to_all(copies, BLK, 0, 0)  7.48 us
    all_to_all x1, waiting for transfers between devices, shards(): qt = lax.all_to_all(copies, BLK, 0, 0)  4.63 us
    ppermute x1, starting transfers between devices, shards(): twin = lax.ppermute(part, 'core', [(0, 1), (1, 0)])  4.47 us
  transfers between devices with their start and end apart: 2, of which 2 were waited for; matrix products, arithmetic and copies ran while one was open for 0% of the time, Pallas kernels for 4%

profile of v5, /device:TPU:1, one launch (start us, length us, event | category | flops | bytes accessed | tf_op | source)
XLA Modules:
  0.0 77.0 jit_solution(10188576166809259605)
XLA Ops:
  0.6 2.0 %query_tokens.1 = bf16[8,128,128]{2,1,0:T(8,128)(2,1)} custom-call(bf16[128,768]{1,0:T(8,128)(2,1)} %bitcast.6, bf16[768,128]{1,0:T(8,128)(2,1)} %w_ref.1), custom_call_target="tpu_custom_call" | custom-call | flops 25165824 | bytes 400000 | tf_op jit(solution)/shard_map/query_tokens/pallas_call | solution.py:262
  2.6 7.5 %all-to-all-start = ((bf16[8,128,128]{2,1,0:T(8,128)(2,1)}), bf16[8,128,128]{2,1,0:T(8,128)(2,1)S(1)}, u32[]{:S(2)}, u32[]{:S(2)}) async-start(bf16[8,128,128]{2,1,0:T(8,128)(2,1)} %query_tokens.1), calls=%async_computation | async-start | bytes 524288 | tf_op jit(solution)/shard_map/all_to_all | solution.py:342
  10.1 2.9 %passage_tokens.1 = (bf16[4,2,512,128]{3,2,1,0:T(8,128)(2,1)S(1)}, s32[5,8,128]{2,1,0:T(8,128)S(1)}) custom-call(s32[1,4]{1,0:T(1,128)} %len_hbm.1, bf16[4,512,768]{2,1,0:T(8,128)(2,1)} %bitcast.8, bf16[768,128]{1,0:T(8,128)(2,1)} %w_ref.1), custom_call_target="tpu_custom_call" | custom-call | flops 402653184 | bytes 8000000 | tf_op jit(solution)/shard_map/passage_tokens/pallas_call | solution.py:262
  13.0 0.0 copy-start
  13.1 4.6 %all-to-all-done.qt_ref = bf16[8,128,128]{2,1,0:T(8,128)(2,1)S(1)} async-done(((bf16[8,128,128]{2,1,0:T(8,128)(2,1)}), bf16[8,128,128]{2,1,0:T(8,128)(2,1)S(1)}, u32[]{:S(2)}, u32[]{:S(2)}) %all-to-all-start) | async-done | bytes 262176 | tf_op jit(solution)/shard_map/all_to_all | solution.py:342
  17.7 4.0 %scores.1 = (bf16[4,512,1024]{2,1,0:T(8,128)(2,1)S(1)}, f32[2,4,8,128]{3,2,1,0:T(8,128)S(1)}, bf16[8,136,128]{2,1,0:T(8,128)(2,1)S(1)}, f32[4,128,128]{2,1,0:T(8,128)S(1)}, bf16[4,512,768]{2,1,0:T(8,128)(2,1)S(1)}) custom-call(bf16[8,128,128]{2,1,0:T(8,128)(2,1)S(1)} %all-to-all-done.qt_ref, bf16[4,2,512,128]{3,2,1,0:T(8,128)(2,1)S(1)} %get-tuple-element.19.tok_ref, ...), custom_call_target="tpu_custom_call" | custom-call | flops 1073741824 | bytes 8000000 | tf_op jit(solution)/shard_map/scores/pallas_call | solution.py:262
  21.7 10.6 %all_to_all.25.recv_ref = bf16[8,136,128]{2,1,0:T(8,128)(2,1)S(1)} all-to-all(bf16[8,136,128]{2,1,0:T(8,128)(2,1)S(1)} %get-tuple-element.20), channel_id=1, replica_groups=mesh['x_hi'=2,'y'=4,'z'=8,'x_lo'=2,'core'=2] {'x_hi','y'}, dimensions={0} | all-to-all | bytes 557056 | tf_op jit(solution)/shard_map/all_to_all | solution.py:345
  32.3 0.0 copy-done
  32.3 3.1 %grads.1 = (f32[128,128]{1,0:T(8,128)}, f32[4,512,128]{2,1,0:T(8,128)}, bf16[16,56,128]{2,1,0:T(8,128)(2,1)S(1)}) custom-call(s32[5,8,128]{2,1,0:T(8,128)S(1)} %get-tuple-element.18.tab_ref, bf16[8,136,128]{2,1,0:T(8,128)(2,1)S(1)} %all_to_all.25.recv_ref, bf16[4,512,1024]{2,1,0:T(8,128)(2,1)S(1)} %get-tuple-element.21.e_ref, ...), custom_call_target="tpu_custom_call" | custom-call | flops 536870912 | bytes 8000000 | tf_op jit(solution)/shard_map/grads/pallas_call | solution.py:262
  35.4 9.9 %all_to_all.26.x_ref = bf16[16,56,128]{2,1,0:T(8,128)(2,1)S(1)} all-to-all(bf16[16,56,128]{2,1,0:T(8,128)(2,1)S(1)} %get-tuple-element.27), channel_id=1, replica_groups=mesh['x_hi'=2,'y'=4,'z'=8,'x_lo'=2,'core'=2] {'x_hi','y','x_lo'}, dimensions={0} | all-to-all | bytes 458752 | tf_op jit(solution)/shard_map/all_to_all | solution.py:347
  45.4 4.5 %collective-permute-start = (f32[56,128]{1,0:T(8,128)S(1)}, f32[56,128]{1,0:T(8,128)S(1)}, u32[]{:S(2)}, u32[]{:S(2)}) collective-permute-start(f32[56,128]{1,0:T(8,128)S(1)} %sum_plane.1.x_ref), channel_id=1, source_target_pairs={{0,1},{1,0},{2,3},{3,2},{4,5},{5,4},{6,7},{7,6},{8,9},{9,8},{10,11... | collective-permute-start | bytes 86024 | tf_op jit(solution)/shard_map/ppermute | solution.py:349
  49.8 0.9 %collective-permute-done.y_ref = f32[56,128]{1,0:T(8,128)S(1)} collective-permute-done((f32[56,128]{1,0:T(8,128)S(1)}, f32[56,128]{1,0:T(8,128)S(1)}, u32[]{:S(2)}, u32[]{:S(2)}) %collective-permute-start) | collective-permute-done | bytes 28704 | tf_op jit(solution)/shard_map/ppermute | solution.py:349
  50.7 15.6 %all_to_all.27.x_ref = bf16[8,56,128]{2,1,0:T(8,128)(2,1)S(1)} all-to-all(bf16[8,56,128]{2,1,0:T(8,128)(2,1)S(1)} %sum_pair.1), channel_id=1, replica_groups=mesh['x_hi'=2,'y'=4,'z'=8,'x_lo'=2,'core'=2] {'z'}, dimensions={0} | all-to-all | bytes 229376 | tf_op jit(solution)/shard_map/all_to_all | solution.py:351
  66.3 9.9 %all_to_all.28.x_ref = bf16[16,48,128]{2,1,0:T(8,128)(2,1)S(1)} all-to-all(bf16[16,48,128]{2,1,0:T(8,128)(2,1)S(1)} %get-tuple-element.28), channel_id=1, replica_groups=mesh['x_hi'=2,'y'=4,'z'=8,'x_lo'=2,'core'=2] {'x_hi','y','x_lo'}, dimensions={0} | all-to-all | bytes 393216 | tf_op jit(solution)/shard_map/all_to_all | solution.py:356
  76.2 0.8 %final.1 = (f32[768,128]{1,0:T(8,128)}, f32[1,128]{1,0:T(1,128)}) custom-call(bf16[16,48,128]{2,1,0:T(8,128)(2,1)S(1)} %all_to_all.28.x_ref, f32[8,128]{1,0:T(8,128)S(1)} %get-tuple-element.29.loss_in_ref), custom_call_target="tpu_custom_call" | custom-call | tf_op jit(solution)/shard_map/final/pallas_call | solution.py:262
  (3 shorter events, 0.1 us)
Async XLA Ops:
  2.6 15.1 %all-to-all-start = ((bf16[8,128,128]{2,1,0:T(8,128)(2,1)}), bf16[8,128,128]{2,1,0:T(8,128)(2,1)S(1)}, u32[]{:S(2)}, u32[]{:S(2)}) async-start(bf16[8,128,128]{2,1,0:T(8,128)(2,1)} %query_tokens.1), calls=%async_computation | async-start | bytes 524288 | tf_op jit(solution)/shard_map/all_to_all | solution.py:342
  13.0 19.2 %copy-start = (bf16[1,4,32,768]{3,2,1,0:T(8,128)(2,1)S(1)}, bf16[1,4,32,768]{3,2,1,0:T(8,128)(2,1)}, u32[]{:S(2)}) copy-start(bf16[1,4,32,768]{3,2,1,0:T(8,128)(2,1)} %param.4) | copy-start | bytes 589828
  45.4 5.3 %collective-permute-start = (f32[56,128]{1,0:T(8,128)S(1)}, f32[56,128]{1,0:T(8,128)S(1)}, u32[]{:S(2)}, u32[]{:S(2)}) collective-permute-start(f32[56,128]{1,0:T(8,128)S(1)} %sum_plane.1.x_ref), channel_id=1, source_target_pairs={{0,1},{1,0},{2,3},{3,2},{4,5},{5,4},{6,7},{7,6},{8,9},{9,8},{10,11... | collective-permute-start | bytes 86024 | tf_op jit(solution)/shard_map/ppermute | solution.py:349

commit v6 on v5

--- a/solution.py
+++ b/solution.py
@@ -93,7 +93,7 @@
 
 def score_kernel(
     qlen, qt_ref, tok_ref, tab_ref, phid_hbm, e_ref, stat_ref, send_ref, own_ref, phid_ref,
-    qs_ref, s_ref, g_ref, sem,
+    qs_ref, s_ref, g_ref, top_ref, sem,
 ):
     copies = [
         pltpu.make_async_copy(phid_hbm, phid_ref, sem.at[0]),
@@ -123,10 +123,12 @@
 
     def powers(p, top):
         total = jnp.zeros((8, ntok), F32)
+        top_ref[...] = jnp.broadcast_to(top, (8, ntok))
+        wide = top_ref[...]
         for r in range(0, slots, 16):
-            e = jnp.exp2((s_ref[p % 2, r : r + 16, :] - top) * EXP2_SCALE)
-            total = total + fold(e, jnp.add)
-            e_ref[p, r : r + 16, :] = e.astype(BF16)
+            parts = [jnp.exp2((s_ref[p % 2, q : q + 8, :] - wide) * EXP2_SCALE) for q in (r, r + 8)]
+            total = total + (parts[0] + parts[1])
+            e_ref[p, r : r + 16, :] = jnp.concatenate(parts, axis=0).astype(BF16)
         return jnp.sum(total, axis=0, keepdims=True)
 
     def finish(p, top, total):
@@ -227,7 +229,19 @@
     out_ref[...] = jnp.sum(x_ref[...].astype(F32), axis=0)
 
 
-def sum_pair_kernel(x_ref, y_ref, out_ref):
+def write_kernel(qgrad_ref, pgrad_ref, after_ref, qgrad_hbm, pgrad_hbm, done_ref, sem):
+    copies = [
+        pltpu.make_async_copy(qgrad_ref, qgrad_hbm, sem.at[0]),
+        pltpu.make_async_copy(pgrad_ref, pgrad_hbm, sem.at[1]),
+    ]
+    for copy in copies:
+        copy.start()
+    done_ref[...] = after_ref[:8, :]
+    for copy in copies:
+        copy.wait()
+
+
+def sum_pair_kernel(x_ref, y_ref, done_ref, out_ref):
     y = x_ref[...] + y_ref[...]
     rows = y.shape[0] - 8
     hi, mid, lo = split3(jnp.sum(y[rows:], axis=0, keepdims=True))
@@ -305,7 +319,8 @@
          S((npass, dim, LANES), F32), S(phid.shape, BF16)),
         qt, tok, tab, phid,
         scratch=[pltpu.VMEM((dim, ntok), BF16), pltpu.VMEM((2, plen, ntok), F32),
-                 pltpu.VMEM((npass, nblk, dim, LANES), F32), pltpu.SemaphoreType.DMA((2,))],
+                 pltpu.VMEM((npass, nblk, dim, LANES), F32), pltpu.VMEM((8, ntok), F32),
+                 pltpu.SemaphoreType.DMA((2,))],
         flops=4 * npass * plen * ntok * dim, bytes_accessed=8_000_000,
     )
 
@@ -318,7 +333,7 @@
     S = jax.ShapeDtypeStruct
     return call(
         "grads", functools.partial(grad_kernel, qlen, total), [VM] * 8,
-        (S((mine, dim), F32), S((npass, plen, dim), F32), S((nplane, rows + 8, dim), BF16)),
+        (pltpu.VMEM((mine, dim), F32), pltpu.VMEM((npass, plen, dim), F32), S((nplane, rows + 8, dim), BF16)),
         tab, recv, e, stat, own, qt, phid, qhid,
         scratch=[pltpu.VMEM((dim, hidden), F32), pltpu.VMEM((2, dim, ntok), BF16), pltpu.VMEM((npass * plen, dim), BF16)],
         flops=2 * npass * plen * ntok * dim, bytes_accessed=8_000_000,
@@ -347,7 +362,12 @@
     part = lax.all_to_all(send, PLANE, 0, 0)
     part = call("sum_plane", sum_plane_kernel, [VM], S((rows + 8, dim), F32), part)
     twin = lax.ppermute(part, "core", [(0, 1), (1, 0)])
-    part = call("sum_pair", sum_pair_kernel, [VM, VM], S((ncolumn, rows + 8, dim), BF16), part, twin)
+    qgrad, pgrad, done = call(
+        "write_out", write_kernel, [VM, VM, VM],
+        (S((mine, dim), F32), S((npass, plen, dim), F32), S((8, dim), F32)), qgrad, pgrad, part,
+        outs=(HBM, HBM, VM), scratch=[pltpu.SemaphoreType.DMA((2,))], bytes_accessed=2_000_000,
+    )
+    part = call("sum_pair", sum_pair_kernel, [VM, VM, VM], S((ncolumn, rows + 8, dim), BF16), part, twin, done)
     part = lax.all_to_all(part, COLUMN, 0, 0)
     part, loss = call(
         "sum_column", functools.partial(sum_column_kernel, float(total)), [VM],

time: 78.4 us -> 78 us (level)
  waiting for transfers between devices: 5.48 us -> 4.63 us
    ppermute x1, waiting for transfers between devices: 0.85 us -> 0.01 us  [shards(): twin = lax.ppermute(part, 'core', [(0, 1), (1, 0)])]
    pallas_call x8 -> x9, Pallas kernels: 12.9 us -> 13.3 us  [call(): pl.pallas_call(kernel, name=name, out_shape=out_shape, in_specs=ins, out_...]
  transfers between devices with their start and end apart: 2 -> 2, of which waited for: 2 -> 1; matrix products, arithmetic and copies ran while one was open for 0% -> 0% of each run, Pallas kernels for 4% -> 5%
where the time goes in v6:
time: 78 us; the launch traced here: 76.9 us
  blocking collectives  46.3 us (59%)
  Pallas kernels  13.3 us (17%)
  starting transfers between devices  11.9 us (15%)
  waiting for transfers between devices  4.63 us (6%)
    all_to_all x1, blocking collectives, shards(): part = lax.all_to_all(part, COLUMN, 0, 0)  15.9 us
    pallas_call x9, Pallas kernels, call(): pl.pallas_call(kernel, name=name, out_shape=out_shape, in_specs=ins, out_...  13.3 us
    all_to_all x1, blocking collectives, shards(): recv = lax.all_to_all(send, BLK, 0, 0)  10.6 us
    all_to_all x1, blocking collectives, shards(): part = lax.all_to_all(send, PLANE, 0, 0)  9.96 us
    all_to_all x1, blocking collectives, shards(): part = lax.all_to_all(part, PLANE, 0, 0)  9.86 us
    all_to_all x1, starting transfers between devices, shards(): qt = lax.all_to_all(copies, BLK, 0, 0)  7.48 us
    all_to_all x1, waiting for transfers between devices, shards(): qt = lax.all_to_all(copies, BLK, 0, 0)  4.63 us
    ppermute x1, starting transfers between devices, shards(): twin = lax.ppermute(part, 'core', [(0, 1), (1, 0)])  4.46 us
  transfers between devices with their start and end apart: 2, of which 1 were waited for; matrix products, arithmetic and copies ran while one was open for 0% of the time, Pallas kernels for 5%

profile of v6, /device:TPU:1, one launch (start us, length us, event | category | flops | bytes accessed | tf_op | source)
XLA Modules:
  0.0 76.9 jit_solution(14005856771464659955)
XLA Ops:
  0.6 2.0 %query_tokens.1 = bf16[8,128,128]{2,1,0:T(8,128)(2,1)} custom-call(bf16[128,768]{1,0:T(8,128)(2,1)} %bitcast.6, bf16[768,128]{1,0:T(8,128)(2,1)} %w_ref.1), custom_call_target="tpu_custom_call" | custom-call | flops 25165824 | bytes 400000 | tf_op jit(solution)/shard_map/query_tokens/pallas_call | solution.py:276
  2.6 7.5 %all-to-all-start = ((bf16[8,128,128]{2,1,0:T(8,128)(2,1)}), bf16[8,128,128]{2,1,0:T(8,128)(2,1)S(1)}, u32[]{:S(2)}, u32[]{:S(2)}) async-start(bf16[8,128,128]{2,1,0:T(8,128)(2,1)} %query_tokens.1), calls=%async_computation | async-start | bytes 524288 | tf_op jit(solution)/shard_map/all_to_all | solution.py:357
  10.1 2.9 %passage_tokens.1 = (bf16[4,2,512,128]{3,2,1,0:T(8,128)(2,1)S(1)}, s32[5,8,128]{2,1,0:T(8,128)S(1)}) custom-call(s32[1,4]{1,0:T(1,128)} %len_hbm.1, bf16[4,512,768]{2,1,0:T(8,128)(2,1)} %bitcast.8, bf16[768,128]{1,0:T(8,128)(2,1)} %w_ref.1), custom_call_target="tpu_custom_call" | custom-call | flops 402653184 | bytes 8000000 | tf_op jit(solution)/shard_map/passage_tokens/pallas_call | solution.py:276
  13.0 0.0 copy-start
  13.1 4.6 %all-to-all-done.qt_ref = bf16[8,128,128]{2,1,0:T(8,128)(2,1)S(1)} async-done(((bf16[8,128,128]{2,1,0:T(8,128)(2,1)}), bf16[8,128,128]{2,1,0:T(8,128)(2,1)S(1)}, u32[]{:S(2)}, u32[]{:S(2)}) %all-to-all-start) | async-done | bytes 262176 | tf_op jit(solution)/shard_map/all_to_all | solution.py:357
  17.7 4.0 %scores.1 = (bf16[4,512,1024]{2,1,0:T(8,128)(2,1)S(1)}, f32[2,4,8,128]{3,2,1,0:T(8,128)S(1)}, bf16[8,136,128]{2,1,0:T(8,128)(2,1)S(1)}, f32[4,128,128]{2,1,0:T(8,128)S(1)}, bf16[4,512,768]{2,1,0:T(8,128)(2,1)S(1)}) custom-call(bf16[8,128,128]{2,1,0:T(8,128)(2,1)S(1)} %all-to-all-done.qt_ref, bf16[4,2,512,128]{3,2,1,0:T(8,128)(2,1)S(1)} %get-tuple-element.22.tok_ref, ...), custom_call_target="tpu_custom_call" | custom-call | flops 1073741824 | bytes 8000000 | tf_op jit(solution)/shard_map/scores/pallas_call | solution.py:276
  21.7 10.6 %all_to_all.25.recv_ref = bf16[8,136,128]{2,1,0:T(8,128)(2,1)S(1)} all-to-all(bf16[8,136,128]{2,1,0:T(8,128)(2,1)S(1)} %get-tuple-element.23), channel_id=1, replica_groups=mesh['x_hi'=2,'y'=4,'z'=8,'x_lo'=2,'core'=2] {'x_hi','y'}, dimensions={0} | all-to-all | bytes 557056 | tf_op jit(solution)/shard_map/all_to_all | solution.py:360
  32.3 0.0 copy-done
  32.3 2.5 %grads.1 = (f32[128,128]{1,0:T(8,128)S(1)}, f32[4,512,128]{2,1,0:T(8,128)S(1)}, bf16[16,56,128]{2,1,0:T(8,128)(2,1)S(1)}) custom-call(s32[5,8,128]{2,1,0:T(8,128)S(1)} %get-tuple-element.21.tab_ref, bf16[8,136,128]{2,1,0:T(8,128)(2,1)S(1)} %all_to_all.25.recv_ref, bf16[4,512,1024]{2,1,0:T(8,128)(2,1)S(1)} %get-tuple-element.24.e_ref, ...), custom_call_target="tpu_custom_call" | custom-call | flops 536870912 | bytes 8000000 | tf_op jit(solution)/shard_map/grads/pallas_call | solution.py:276
  34.9 10.0 %all_to_all.26.x_ref = bf16[16,56,128]{2,1,0:T(8,128)(2,1)S(1)} all-to-all(bf16[16,56,128]{2,1,0:T(8,128)(2,1)S(1)} %get-tuple-element.30), channel_id=1, replica_groups=mesh['x_hi'=2,'y'=4,'z'=8,'x_lo'=2,'core'=2] {'x_hi','y','x_lo'}, dimensions={0} | all-to-all | bytes 458752 | tf_op jit(solution)/shard_map/all_to_all | solution.py:362
  44.9 4.5 %collective-permute-start = (f32[56,128]{1,0:T(8,128)S(1)}, f32[56,128]{1,0:T(8,128)S(1)}, u32[]{:S(2)}, u32[]{:S(2)}) collective-permute-start(f32[56,128]{1,0:T(8,128)S(1)} %sum_plane.1.after_ref.x_ref), channel_id=1, source_target_pairs={{0,1},{1,0},{2,3},{3,2},{4,5},{5,4},{6,7},{7,6},{8,9},{9,8},{10,11... | collective-permute-start | bytes 86024 | tf_op jit(solution)/shard_map/ppermute | solution.py:364
  49.3 1.0 %write_out.1 = (f32[128,128]{1,0:T(8,128)}, f32[4,512,128]{2,1,0:T(8,128)}, f32[8,128]{1,0:T(8,128)S(1)}) custom-call(f32[128,128]{1,0:T(8,128)S(1)} %get-tuple-element.28.qgrad_ref, f32[4,512,128]{2,1,0:T(8,128)S(1)} %get-tuple-element.29.pgrad_ref, f32[56,128]{1,0:T(8,128)S(1)} %sum_plane.1.after_ref.x_ref), custom_call_target="tpu_custom_call" | custom-call | bytes 2000000 | tf_op jit(solution)/shard_map/write_out/pallas_call | solution.py:276
  50.3 0.0 collective-permute-done.y_ref
  50.4 15.9 %all_to_all.27.x_ref = bf16[8,56,128]{2,1,0:T(8,128)(2,1)S(1)} all-to-all(bf16[8,56,128]{2,1,0:T(8,128)(2,1)S(1)} %sum_pair.1), channel_id=1, replica_groups=mesh['x_hi'=2,'y'=4,'z'=8,'x_lo'=2,'core'=2] {'z'}, dimensions={0} | all-to-all | bytes 229376 | tf_op jit(solution)/shard_map/all_to_all | solution.py:371
  66.3 9.9 %all_to_all.28.x_ref = bf16[16,48,128]{2,1,0:T(8,128)(2,1)S(1)} all-to-all(bf16[16,48,128]{2,1,0:T(8,128)(2,1)S(1)} %get-tuple-element.34), channel_id=1, replica_groups=mesh['x_hi'=2,'y'=4,'z'=8,'x_lo'=2,'core'=2] {'x_hi','y','x_lo'}, dimensions={0} | all-to-all | bytes 393216 | tf_op jit(solution)/shard_map/all_to_all | solution.py:376
  76.1 0.8 %final.1 = (f32[768,128]{1,0:T(8,128)}, f32[1,128]{1,0:T(1,128)}) custom-call(bf16[16,48,128]{2,1,0:T(8,128)(2,1)S(1)} %all_to_all.28.x_ref, f32[8,128]{1,0:T(8,128)S(1)} %get-tuple-element.35.loss_in_ref), custom_call_target="tpu_custom_call" | custom-call | tf_op jit(solution)/shard_map/final/pallas_call | solution.py:276
  (3 shorter events, 0.1 us)
Async XLA Ops:
  2.6 15.1 %all-to-all-start = ((bf16[8,128,128]{2,1,0:T(8,128)(2,1)}), bf16[8,128,128]{2,1,0:T(8,128)(2,1)S(1)}, u32[]{:S(2)}, u32[]{:S(2)}) async-start(bf16[8,128,128]{2,1,0:T(8,128)(2,1)} %query_tokens.1), calls=%async_computation | async-start | bytes 524288 | tf_op jit(solution)/shard_map/all_to_all | solution.py:357
  13.0 19.3 %copy-start = (bf16[1,4,32,768]{3,2,1,0:T(8,128)(2,1)S(1)}, bf16[1,4,32,768]{3,2,1,0:T(8,128)(2,1)}, u32[]{:S(2)}) copy-start(bf16[1,4,32,768]{3,2,1,0:T(8,128)(2,1)} %param.4) | copy-start | bytes 589828
  44.9 5.5 %collective-permute-start = (f32[56,128]{1,0:T(8,128)S(1)}, f32[56,128]{1,0:T(8,128)S(1)}, u32[]{:S(2)}, u32[]{:S(2)}) collective-permute-start(f32[56,128]{1,0:T(8,128)S(1)} %sum_plane.1.after_ref.x_ref), channel_id=1, source_target_pairs={{0,1},{1,0},{2,3},{3,2},{4,5},{5,4},{6,7},{7,6},{8,9},{9,8},{10,11... | collective-permute-start | bytes 86024 | tf_op jit(solution)/shard_map/ppermute | solution.py:364

commit v7 on v6

--- a/solution.py
+++ b/solution.py
@@ -133,14 +133,14 @@
 
     def finish(p, top, total):
         inv = 1.0 / total
+        logz = to_chunks(top * INV_TEMPER + jnp.log(total))
+        log_count = jnp.log(tab_ref[p].astype(F32))
+        stat_ref[0, p] = segment_sum(TEMPER * (logz - log_count), qlen)
+        stat_ref[1, p] = to_chunks(inv)
         flipped = jnp.concatenate([tok_ref[p, 1, r : r + LANES, :] for r in range(0, slots, LANES)], axis=1)
         g = mm(flipped, e_ref[p], NN) * inv
         for c in range(nblk):
             g_ref[p, c] = g[:, c * LANES : (c + 1) * LANES]
-        logz = to_chunks(top * INV_TEMPER + jnp.log(total))
-        log_count = jnp.log(tab_ref[p].astype(F32))
-        stat_ref[0, p] = segment_sum(TEMPER * (logz - log_count), qlen)
-        stat_ref[1, p] = to_chunks(inv)
 
     top = scores(0)
     for p in range(npass):

time: 78 us -> 78 us (level)
  no operation moved by 1% of the time
where the time goes in v7:
time: 78 us; the launch traced here: 76.9 us
  blocking collectives  46.3 us (59%)
  Pallas kernels  13.3 us (17%)
  starting transfers between devices  11.9 us (15%)
  waiting for transfers between devices  4.63 us (6%)
    all_to_all x1, blocking collectives, shards(): part = lax.all_to_all(part, COLUMN, 0, 0)  15.9 us
    pallas_call x9, Pallas kernels, call(): pl.pallas_call(kernel, name=name, out_shape=out_shape, in_specs=ins, out_...  13.3 us
    all_to_all x1, blocking collectives, shards(): recv = lax.all_to_all(send, BLK, 0, 0)  10.6 us
    all_to_all x1, blocking collectives, shards(): part = lax.all_to_all(send, PLANE, 0, 0)  9.96 us
    all_to_all x1, blocking collectives, shards(): part = lax.all_to_all(part, PLANE, 0, 0)  9.86 us
    all_to_all x1, starting transfers between devices, shards(): qt = lax.all_to_all(copies, BLK, 0, 0)  7.48 us
    all_to_all x1, waiting for transfers between devices, shards(): qt = lax.all_to_all(copies, BLK, 0, 0)  4.63 us
    ppermute x1, starting transfers between devices, shards(): twin = lax.ppermute(part, 'core', [(0, 1), (1, 0)])  4.46 us
  transfers between devices with their start and end apart: 2, of which 1 were waited for; matrix products, arithmetic and copies ran while one was open for 0% of the time, Pallas kernels for 5%

profile of v7, /device:TPU:1, one launch (start us, length us, event | category | flops | bytes accessed | tf_op | source)
XLA Modules:
  0.0 76.9 jit_solution(14005856771464659955)
XLA Ops:
  0.6 2.0 %query_tokens.1 = bf16[8,128,128]{2,1,0:T(8,128)(2,1)} custom-call(bf16[128,768]{1,0:T(8,128)(2,1)} %bitcast.6, bf16[768,128]{1,0:T(8,128)(2,1)} %w_ref.1), custom_call_target="tpu_custom_call" | custom-call | flops 25165824 | bytes 400000 | tf_op jit(solution)/shard_map/query_tokens/pallas_call | solution.py:276
  2.6 7.5 %all-to-all-start = ((bf16[8,128,128]{2,1,0:T(8,128)(2,1)}), bf16[8,128,128]{2,1,0:T(8,128)(2,1)S(1)}, u32[]{:S(2)}, u32[]{:S(2)}) async-start(bf16[8,128,128]{2,1,0:T(8,128)(2,1)} %query_tokens.1), calls=%async_computation | async-start | bytes 524288 | tf_op jit(solution)/shard_map/all_to_all | solution.py:357
  10.1 2.9 %passage_tokens.1 = (bf16[4,2,512,128]{3,2,1,0:T(8,128)(2,1)S(1)}, s32[5,8,128]{2,1,0:T(8,128)S(1)}) custom-call(s32[1,4]{1,0:T(1,128)} %len_hbm.1, bf16[4,512,768]{2,1,0:T(8,128)(2,1)} %bitcast.8, bf16[768,128]{1,0:T(8,128)(2,1)} %w_ref.1), custom_call_target="tpu_custom_call" | custom-call | flops 402653184 | bytes 8000000 | tf_op jit(solution)/shard_map/passage_tokens/pallas_call | solution.py:276
  13.0 0.0 copy-start
  13.1 4.6 %all-to-all-done.qt_ref = bf16[8,128,128]{2,1,0:T(8,128)(2,1)S(1)} async-done(((bf16[8,128,128]{2,1,0:T(8,128)(2,1)}), bf16[8,128,128]{2,1,0:T(8,128)(2,1)S(1)}, u32[]{:S(2)}, u32[]{:S(2)}) %all-to-all-start) | async-done | bytes 262176 | tf_op jit(solution)/shard_map/all_to_all | solution.py:357
  17.7 4.0 %scores.1 = (bf16[4,512,1024]{2,1,0:T(8,128)(2,1)S(1)}, f32[2,4,8,128]{3,2,1,0:T(8,128)S(1)}, bf16[8,136,128]{2,1,0:T(8,128)(2,1)S(1)}, f32[4,128,128]{2,1,0:T(8,128)S(1)}, bf16[4,512,768]{2,1,0:T(8,128)(2,1)S(1)}) custom-call(bf16[8,128,128]{2,1,0:T(8,128)(2,1)S(1)} %all-to-all-done.qt_ref, bf16[4,2,512,128]{3,2,1,0:T(8,128)(2,1)S(1)} %get-tuple-element.22.tok_ref, ...), custom_call_target="tpu_custom_call" | custom-call | flops 1073741824 | bytes 8000000 | tf_op jit(solution)/shard_map/scores/pallas_call | solution.py:276
  21.7 10.6 %all_to_all.25.recv_ref = bf16[8,136,128]{2,1,0:T(8,128)(2,1)S(1)} all-to-all(bf16[8,136,128]{2,1,0:T(8,128)(2,1)S(1)} %get-tuple-element.23), channel_id=1, replica_groups=mesh['x_hi'=2,'y'=4,'z'=8,'x_lo'=2,'core'=2] {'x_hi','y'}, dimensions={0} | all-to-all | bytes 557056 | tf_op jit(solution)/shard_map/all_to_all | solution.py:360
  32.3 0.0 copy-done
  32.3 2.5 %grads.1 = (f32[128,128]{1,0:T(8,128)S(1)}, f32[4,512,128]{2,1,0:T(8,128)S(1)}, bf16[16,56,128]{2,1,0:T(8,128)(2,1)S(1)}) custom-call(s32[5,8,128]{2,1,0:T(8,128)S(1)} %get-tuple-element.21.tab_ref, bf16[8,136,128]{2,1,0:T(8,128)(2,1)S(1)} %all_to_all.25.recv_ref, bf16[4,512,1024]{2,1,0:T(8,128)(2,1)S(1)} %get-tuple-element.24.e_ref, ...), custom_call_target="tpu_custom_call" | custom-call | flops 536870912 | bytes 8000000 | tf_op jit(solution)/shard_map/grads/pallas_call | solution.py:276
  34.9 10.0 %all_to_all.26.x_ref = bf16[16,56,128]{2,1,0:T(8,128)(2,1)S(1)} all-to-all(bf16[16,56,128]{2,1,0:T(8,128)(2,1)S(1)} %get-tuple-element.30), channel_id=1, replica_groups=mesh['x_hi'=2,'y'=4,'z'=8,'x_lo'=2,'core'=2] {'x_hi','y','x_lo'}, dimensions={0} | all-to-all | bytes 458752 | tf_op jit(solution)/shard_map/all_to_all | solution.py:362
  44.9 4.5 %collective-permute-start = (f32[56,128]{1,0:T(8,128)S(1)}, f32[56,128]{1,0:T(8,128)S(1)}, u32[]{:S(2)}, u32[]{:S(2)}) collective-permute-start(f32[56,128]{1,0:T(8,128)S(1)} %sum_plane.1.after_ref.x_ref), channel_id=1, source_target_pairs={{0,1},{1,0},{2,3},{3,2},{4,5},{5,4},{6,7},{7,6},{8,9},{9,8},{10,11... | collective-permute-start | bytes 86024 | tf_op jit(solution)/shard_map/ppermute | solution.py:364
  49.3 1.0 %write_out.1 = (f32[128,128]{1,0:T(8,128)}, f32[4,512,128]{2,1,0:T(8,128)}, f32[8,128]{1,0:T(8,128)S(1)}) custom-call(f32[128,128]{1,0:T(8,128)S(1)} %get-tuple-element.28.qgrad_ref, f32[4,512,128]{2,1,0:T(8,128)S(1)} %get-tuple-element.29.pgrad_ref, f32[56,128]{1,0:T(8,128)S(1)} %sum_plane.1.after_ref.x_ref), custom_call_target="tpu_custom_call" | custom-call | bytes 2000000 | tf_op jit(solution)/shard_map/write_out/pallas_call | solution.py:276
  50.3 0.0 collective-permute-done.y_ref
  50.4 15.9 %all_to_all.27.x_ref = bf16[8,56,128]{2,1,0:T(8,128)(2,1)S(1)} all-to-all(bf16[8,56,128]{2,1,0:T(8,128)(2,1)S(1)} %sum_pair.1), channel_id=1, replica_groups=mesh['x_hi'=2,'y'=4,'z'=8,'x_lo'=2,'core'=2] {'z'}, dimensions={0} | all-to-all | bytes 229376 | tf_op jit(solution)/shard_map/all_to_all | solution.py:371
  66.3 9.9 %all_to_all.28.x_ref = bf16[16,48,128]{2,1,0:T(8,128)(2,1)S(1)} all-to-all(bf16[16,48,128]{2,1,0:T(8,128)(2,1)S(1)} %get-tuple-element.34), channel_id=1, replica_groups=mesh['x_hi'=2,'y'=4,'z'=8,'x_lo'=2,'core'=2] {'x_hi','y','x_lo'}, dimensions={0} | all-to-all | bytes 393216 | tf_op jit(solution)/shard_map/all_to_all | solution.py:376
  76.1 0.8 %final.1 = (f32[768,128]{1,0:T(8,128)}, f32[1,128]{1,0:T(1,128)}) custom-call(bf16[16,48,128]{2,1,0:T(8,128)(2,1)S(1)} %all_to_all.28.x_ref, f32[8,128]{1,0:T(8,128)S(1)} %get-tuple-element.35.loss_in_ref), custom_call_target="tpu_custom_call" | custom-call | tf_op jit(solution)/shard_map/final/pallas_call | solution.py:276
  (3 shorter events, 0.1 us)
Async XLA Ops:
  2.6 15.1 %all-to-all-start = ((bf16[8,128,128]{2,1,0:T(8,128)(2,1)}), bf16[8,128,128]{2,1,0:T(8,128)(2,1)S(1)}, u32[]{:S(2)}, u32[]{:S(2)}) async-start(bf16[8,128,128]{2,1,0:T(8,128)(2,1)} %query_tokens.1), calls=%async_computation | async-start | bytes 524288 | tf_op jit(solution)/shard_map/all_to_all | solution.py:357
  13.0 19.3 %copy-start = (bf16[1,4,32,768]{3,2,1,0:T(8,128)(2,1)S(1)}, bf16[1,4,32,768]{3,2,1,0:T(8,128)(2,1)}, u32[]{:S(2)}) copy-start(bf16[1,4,32,768]{3,2,1,0:T(8,128)(2,1)} %param.4) | copy-start | bytes 589828
  44.9 5.5 %collective-permute-start = (f32[56,128]{1,0:T(8,128)S(1)}, f32[56,128]{1,0:T(8,128)S(1)}, u32[]{:S(2)}, u32[]{:S(2)}) collective-permute-start(f32[56,128]{1,0:T(8,128)S(1)} %sum_plane.1.after_ref.x_ref), channel_id=1, source_target_pairs={{0,1},{1,0},{2,3},{3,2},{4,5},{5,4},{6,7},{7,6},{8,9},{9,8},{10,11... | collective-permute-start | bytes 86024 | tf_op jit(solution)/shard_map/ppermute | solution.py:364

commit v8 on v7

--- a/solution.py
+++ b/solution.py
@@ -174,7 +174,7 @@
 
 def grad_kernel(
     qlen, total, tab_ref, recv_ref, e_ref, stat_ref, own_ref, qt_ref, phid_ref, qhid_ref,
-    qgrad_ref, pgrad_ref, send_ref, acc_ref, qs_ref, small_ref,
+    qgrad_ref, pgrad_ref, send_ref, qs_ref, small_ref,
 ):
     nblk = qt_ref.shape[0]
     npass = stat_ref.shape[1]
@@ -207,7 +207,7 @@
         pgrad = mm(e_ref[p], qs_ref[p % 2], NT)
         pgrad_ref[p] = pgrad
         small_ref[p * pgrad.shape[0] : (p + 1) * pgrad.shape[0], :] = pgrad.astype(BF16)
-    acc_ref[...] = mm(small_ref[...], phid_ref[...].reshape(small_ref.shape[0], -1), TN)
+    terms = mm(small_ref[...], phid_ref[...].reshape(small_ref.shape[0], -1), TN)
     grad = jnp.zeros((LANES, LANES), F32)
     for k in range(npass):
         grad = grad + own_ref[k] * pick(dscore[k])
@@ -215,7 +215,7 @@
         share = jnp.where(me == d, 0.0, pick(jnp.exp(parts[d] - lse)) / total)
         grad = grad + recv_ref[d, :LANES, :].astype(F32) * share
     qgrad_ref[...] = grad.T
-    wgrad = (acc_ref[...] + mm(grad.astype(BF16), qhid_ref[...], NN)).T
+    wgrad = (terms + mm(grad.astype(BF16), qhid_ref[...], NN)).T
 
 
     hi, mid, lo = split3(jnp.full((1, LANES), jnp.sum(loss)))
@@ -335,7 +335,7 @@
         "grads", functools.partial(grad_kernel, qlen, total), [VM] * 8,
         (pltpu.VMEM((mine, dim), F32), pltpu.VMEM((npass, plen, dim), F32), S((nplane, rows + 8, dim), BF16)),
         tab, recv, e, stat, own, qt, phid, qhid,
-        scratch=[pltpu.VMEM((dim, hidden), F32), pltpu.VMEM((2, dim, ntok), BF16), pltpu.VMEM((npass * plen, dim), BF16)],
+        scratch=[pltpu.VMEM((2, dim, ntok), BF16), pltpu.VMEM((npass * plen, dim), BF16)],
         flops=2 * npass * plen * ntok * dim, bytes_accessed=8_000_000,
     )
 

time: 78 us -> 78 us (level)
  no operation moved by 1% of the time
where the time goes in v8:
time: 78 us; the launch traced here: 76.8 us
  blocking collectives  46.3 us (59%)
  Pallas kernels  13.3 us (17%)
  starting transfers between devices  11.9 us (15%)
  waiting for transfers between devices  4.63 us (6%)
    all_to_all x1, blocking collectives, shards(): part = lax.all_to_all(part, COLUMN, 0, 0)  15.9 us
    pallas_call x9, Pallas kernels, call(): pl.pallas_call(kernel, name=name, out_shape=out_shape, in_specs=ins, out_...  13.3 us
    all_to_all x1, blocking collectives, shards(): recv = lax.all_to_all(send, BLK, 0, 0)  10.6 us
    all_to_all x1, blocking collectives, shards(): part = lax.all_to_all(send, PLANE, 0, 0)  9.96 us
    all_to_all x1, blocking collectives, shards(): part = lax.all_to_all(part, PLANE, 0, 0)  9.86 us
    all_to_all x1, starting transfers between devices, shards(): qt = lax.all_to_all(copies, BLK, 0, 0)  7.48 us
    all_to_all x1, waiting for transfers between devices, shards(): qt = lax.all_to_all(copies, BLK, 0, 0)  4.63 us
    ppermute x1, starting transfers between devices, shards(): twin = lax.ppermute(part, 'core', [(0, 1), (1, 0)])  4.46 us
  transfers between devices with their start and end apart: 2, of which 1 were waited for; matrix products, arithmetic and copies ran while one was open for 0% of the time, Pallas kernels for 5%

profile of v8, /device:TPU:1, one launch (start us, length us, event | category | flops | bytes accessed | tf_op | source)
XLA Modules:
  0.0 76.8 jit_solution(5593988270920667381)
XLA Ops:
  0.6 2.0 %query_tokens.1 = bf16[8,128,128]{2,1,0:T(8,128)(2,1)} custom-call(bf16[128,768]{1,0:T(8,128)(2,1)} %bitcast.6, bf16[768,128]{1,0:T(8,128)(2,1)} %w_ref.1), custom_call_target="tpu_custom_call" | custom-call | flops 25165824 | bytes 400000 | tf_op jit(solution)/shard_map/query_tokens/pallas_call | solution.py:276
  2.6 7.5 %all-to-all-start = ((bf16[8,128,128]{2,1,0:T(8,128)(2,1)}), bf16[8,128,128]{2,1,0:T(8,128)(2,1)S(1)}, u32[]{:S(2)}, u32[]{:S(2)}) async-start(bf16[8,128,128]{2,1,0:T(8,128)(2,1)} %query_tokens.1), calls=%async_computation | async-start | bytes 524288 | tf_op jit(solution)/shard_map/all_to_all | solution.py:357
  10.1 2.9 %passage_tokens.1 = (bf16[4,2,512,128]{3,2,1,0:T(8,128)(2,1)S(1)}, s32[5,8,128]{2,1,0:T(8,128)S(1)}) custom-call(s32[1,4]{1,0:T(1,128)} %len_hbm.1, bf16[4,512,768]{2,1,0:T(8,128)(2,1)} %bitcast.8, bf16[768,128]{1,0:T(8,128)(2,1)} %w_ref.1), custom_call_target="tpu_custom_call" | custom-call | flops 402653184 | bytes 8000000 | tf_op jit(solution)/shard_map/passage_tokens/pallas_call | solution.py:276
  13.0 0.0 copy-start
  13.1 4.6 %all-to-all-done.qt_ref = bf16[8,128,128]{2,1,0:T(8,128)(2,1)S(1)} async-done(((bf16[8,128,128]{2,1,0:T(8,128)(2,1)}), bf16[8,128,128]{2,1,0:T(8,128)(2,1)S(1)}, u32[]{:S(2)}, u32[]{:S(2)}) %all-to-all-start) | async-done | bytes 262176 | tf_op jit(solution)/shard_map/all_to_all | solution.py:357
  17.7 4.0 %scores.1 = (bf16[4,512,1024]{2,1,0:T(8,128)(2,1)S(1)}, f32[2,4,8,128]{3,2,1,0:T(8,128)S(1)}, bf16[8,136,128]{2,1,0:T(8,128)(2,1)S(1)}, f32[4,128,128]{2,1,0:T(8,128)S(1)}, bf16[4,512,768]{2,1,0:T(8,128)(2,1)S(1)}) custom-call(bf16[8,128,128]{2,1,0:T(8,128)(2,1)S(1)} %all-to-all-done.qt_ref, bf16[4,2,512,128]{3,2,1,0:T(8,128)(2,1)S(1)} %get-tuple-element.22.tok_ref, ...), custom_call_target="tpu_custom_call" | custom-call | flops 1073741824 | bytes 8000000 | tf_op jit(solution)/shard_map/scores/pallas_call | solution.py:276
  21.7 10.6 %all_to_all.25.recv_ref = bf16[8,136,128]{2,1,0:T(8,128)(2,1)S(1)} all-to-all(bf16[8,136,128]{2,1,0:T(8,128)(2,1)S(1)} %get-tuple-element.23), channel_id=1, replica_groups=mesh['x_hi'=2,'y'=4,'z'=8,'x_lo'=2,'core'=2] {'x_hi','y'}, dimensions={0} | all-to-all | bytes 557056 | tf_op jit(solution)/shard_map/all_to_all | solution.py:360
  32.3 0.0 copy-done
  32.3 2.5 %grads.1 = (f32[128,128]{1,0:T(8,128)S(1)}, f32[4,512,128]{2,1,0:T(8,128)S(1)}, bf16[16,56,128]{2,1,0:T(8,128)(2,1)S(1)}) custom-call(s32[5,8,128]{2,1,0:T(8,128)S(1)} %get-tuple-element.21.tab_ref, bf16[8,136,128]{2,1,0:T(8,128)(2,1)S(1)} %all_to_all.25.recv_ref, bf16[4,512,1024]{2,1,0:T(8,128)(2,1)S(1)} %get-tuple-element.24.e_ref, ...), custom_call_target="tpu_custom_call" | custom-call | flops 536870912 | bytes 8000000 | tf_op jit(solution)/shard_map/grads/pallas_call | solution.py:276
  34.8 10.0 %all_to_all.26.x_ref = bf16[16,56,128]{2,1,0:T(8,128)(2,1)S(1)} all-to-all(bf16[16,56,128]{2,1,0:T(8,128)(2,1)S(1)} %get-tuple-element.30), channel_id=1, replica_groups=mesh['x_hi'=2,'y'=4,'z'=8,'x_lo'=2,'core'=2] {'x_hi','y','x_lo'}, dimensions={0} | all-to-all | bytes 458752 | tf_op jit(solution)/shard_map/all_to_all | solution.py:362
  44.8 4.5 %collective-permute-start = (f32[56,128]{1,0:T(8,128)S(1)}, f32[56,128]{1,0:T(8,128)S(1)}, u32[]{:S(2)}, u32[]{:S(2)}) collective-permute-start(f32[56,128]{1,0:T(8,128)S(1)} %sum_plane.1.after_ref.x_ref), channel_id=1, source_target_pairs={{0,1},{1,0},{2,3},{3,2},{4,5},{5,4},{6,7},{7,6},{8,9},{9,8},{10,11... | collective-permute-start | bytes 86024 | tf_op jit(solution)/shard_map/ppermute | solution.py:364
  49.2 1.0 %write_out.1 = (f32[128,128]{1,0:T(8,128)}, f32[4,512,128]{2,1,0:T(8,128)}, f32[8,128]{1,0:T(8,128)S(1)}) custom-call(f32[128,128]{1,0:T(8,128)S(1)} %get-tuple-element.28.qgrad_ref, f32[4,512,128]{2,1,0:T(8,128)S(1)} %get-tuple-element.29.pgrad_ref, f32[56,128]{1,0:T(8,128)S(1)} %sum_plane.1.after_ref.x_ref), custom_call_target="tpu_custom_call" | custom-call | bytes 2000000 | tf_op jit(solution)/shard_map/write_out/pallas_call | solution.py:276
  50.3 0.0 collective-permute-done.y_ref
  50.3 15.9 %all_to_all.27.x_ref = bf16[8,56,128]{2,1,0:T(8,128)(2,1)S(1)} all-to-all(bf16[8,56,128]{2,1,0:T(8,128)(2,1)S(1)} %sum_pair.1), channel_id=1, replica_groups=mesh['x_hi'=2,'y'=4,'z'=8,'x_lo'=2,'core'=2] {'z'}, dimensions={0} | all-to-all | bytes 229376 | tf_op jit(solution)/shard_map/all_to_all | solution.py:371
  66.2 9.9 %all_to_all.28.x_ref = bf16[16,48,128]{2,1,0:T(8,128)(2,1)S(1)} all-to-all(bf16[16,48,128]{2,1,0:T(8,128)(2,1)S(1)} %get-tuple-element.34), channel_id=1, replica_groups=mesh['x_hi'=2,'y'=4,'z'=8,'x_lo'=2,'core'=2] {'x_hi','y','x_lo'}, dimensions={0} | all-to-all | bytes 393216 | tf_op jit(solution)/shard_map/all_to_all | solution.py:376
  76.0 0.8 %final.1 = (f32[768,128]{1,0:T(8,128)}, f32[1,128]{1,0:T(1,128)}) custom-call(bf16[16,48,128]{2,1,0:T(8,128)(2,1)S(1)} %all_to_all.28.x_ref, f32[8,128]{1,0:T(8,128)S(1)} %get-tuple-element.35.loss_in_ref), custom_call_target="tpu_custom_call" | custom-call | tf_op jit(solution)/shard_map/final/pallas_call | solution.py:276
  (3 shorter events, 0.1 us)
Async XLA Ops:
  2.6 15.1 %all-to-all-start = ((bf16[8,128,128]{2,1,0:T(8,128)(2,1)}), bf16[8,128,128]{2,1,0:T(8,128)(2,1)S(1)}, u32[]{:S(2)}, u32[]{:S(2)}) async-start(bf16[8,128,128]{2,1,0:T(8,128)(2,1)} %query_tokens.1), calls=%async_computation | async-start | bytes 524288 | tf_op jit(solution)/shard_map/all_to_all | solution.py:357
  13.0 19.3 %copy-start = (bf16[1,4,32,768]{3,2,1,0:T(8,128)(2,1)S(1)}, bf16[1,4,32,768]{3,2,1,0:T(8,128)(2,1)}, u32[]{:S(2)}) copy-start(bf16[1,4,32,768]{3,2,1,0:T(8,128)(2,1)} %param.4) | copy-start | bytes 589828
  44.8 5.5 %collective-permute-start = (f32[56,128]{1,0:T(8,128)S(1)}, f32[56,128]{1,0:T(8,128)S(1)}, u32[]{:S(2)}, u32[]{:S(2)}) collective-permute-start(f32[56,128]{1,0:T(8,128)S(1)} %sum_plane.1.after_ref.x_ref), channel_id=1, source_target_pairs={{0,1},{1,0},{2,3},{3,2},{4,5},{5,4},{6,7},{7,6},{8,9},{9,8},{10,11... | collective-permute-start | bytes 86024 | tf_op jit(solution)/shard_map/ppermute | solution.py:364
